TPU v7x, 128 devices: a whole 4x4x4 slice. The times are simulated.
128 devices in a mesh: row: 8 (over y, x_hi), col: 16 (over z, x_lo, core).
Axes of the slice: x: 4 (x_hi: 2, x_lo: 2; x = x_hi * 2 + x_lo), y: 4, z: 4, core: 2. Of those that a mesh axis runs over, the one named last changes fastest.
Arguments:
- a_blocks: bfloat16 [16, 8, 16, 32, 128], P('col', 'row'), may hold values from -1 to 1
- a_scale: float32 [16, 8, 16, 4], P('col', 'row'), may hold values from 0.25 to 4
- a_cols: int32 [16, 8, 16, 4], P('col', 'row'), may hold values from 0 to 511, as said below
- b_blocks: bfloat16 [16, 8, 512, 32, 128], P('col', 'row'), may hold values from -1 to 1
- b_scale: float32 [16, 8, 512, 4], P('col', 'row'), may hold values from 0.25 to 4
- b_cols: int32 [16, 8, 512, 4], P('col', 'row'), may hold values from 0 to 511, as said below
Outputs:
- product: bfloat16 [16, 8, 8, 32, 16384], P('col', 'row')
Inputs may be any that keep to these rules, and one draw needn't show every extreme that they name: `a_cols`: the 4 columns of each block row are distinct. `b_cols`: the 4 columns of each block row are distinct.
All inputs are finite; a program needn't handle non-finite values.
Results may differ from a plain program's by a relative error of at most 0.0034.
Values may be sent and summed in bfloat16 or wider, within the bound.
A program may use at most 192 MiB of HBM per device.

v0:
```python
import jax
import jax.numpy as jnp
from jax import lax
from jax.sharding import PartitionSpec as P

JW = 512


def from_behind(shard, axis, by):
    devices = lax.axis_size(axis)
    return lax.ppermute(shard, axis, [(i, (i + by) % devices) for i in range(devices)])


def partner(value, axis, bit):
    mask = 2**bit
    pairs = [(source, source ^ mask) for source in range(lax.axis_size(axis))]
    return lax.ppermute(value, axis, pairs)


def block_sum(total, a_part, a_scl, right, right_scl, right_idx):
    nrows, bsize, _ = a_part.shape
    slots_a = a_scl.shape[1]
    slots_b = right_scl.shape[2]
    left = a_part.reshape(nrows, bsize, slots_a, bsize)
    prods = lax.dot_general(
        left, right, (((3,), (2,)), ((0, 2), (0, 1))), preferred_element_type=jnp.float32
    )
    prods = prods.reshape(nrows, slots_a, bsize, slots_b, bsize)
    prods = jnp.transpose(prods, (0, 1, 3, 2, 4))
    scaled = prods * (a_scl[:, :, None] * right_scl)[..., None, None]
    scaled = scaled.reshape(nrows, slots_a, slots_b, bsize * bsize)
    row_ids = jnp.broadcast_to(jnp.arange(nrows, dtype=jnp.int32)[:, None, None], right_idx.shape)
    return total.at[row_ids, right_idx].add(scaled)


def move_a(a_state):
    a_part, a_scl, a_pos = a_state
    a_part = from_behind(a_part, "row", -1)
    a_scl, a_pos = from_behind((a_scl, a_pos), "row", -1)
    return (a_part, a_scl, a_pos)


def on_device(a_blocks, a_scale, a_cols, b_blocks, b_scale, b_cols):
    ticks = lax.axis_size("row")
    stride = lax.axis_size("col") // ticks
    a_state = (a_blocks[0, 0], a_scale[0, 0], a_cols[0, 0].astype(jnp.float32))
    b_part = b_blocks[0, 0]
    b_scl = b_scale[0, 0]
    b_pos = b_cols[0, 0].astype(jnp.float32)
    nrows = a_blocks.shape[2]
    bsize = a_blocks.shape[3]
    start = jnp.zeros((nrows, JW, bsize * bsize), jnp.float32)

    def apply_state(total, a_now, b_now):
        a_part, a_scl, a_pos = a_now
        held, held_scl, held_pos = b_now
        a_idx = a_pos.astype(jnp.int32)
        rows = jnp.take(held, a_idx, axis=0)
        rows_scl = jnp.take(held_scl, a_idx, axis=0)
        rows_pos = jnp.take(held_pos, a_idx, axis=0).astype(jnp.int32)
        return block_sum(total, a_part, a_scl, rows, rows_scl, rows_pos)

    def advance(step, carry):
        total, a_now, b_now = carry
        total = apply_state(total, a_now, b_now)
        a_now = move_a(a_now)
        held, held_scl, held_pos = b_now
        held = from_behind(held, "col", -stride)
        held_scl, held_pos = from_behind((held_scl, held_pos), "col", -stride)
        return (total, a_now, (held, held_scl, held_pos))

    total, a_state, b_state = lax.fori_loop(
        0, ticks - 1, advance, (start, a_state, (b_part, b_scl, b_pos))
    )
    total = apply_state(total, a_state, b_state)
    rounded = lax.optimization_barrier(total.astype(jnp.bfloat16))
    rounded = rounded.reshape(nrows, JW, bsize, bsize)
    partial_value = jnp.transpose(rounded, (0, 2, 1, 3)).reshape(nrows, bsize, JW * bsize)
    half = nrows // 2
    parity = lax.axis_index("col") % 2
    given = lax.dynamic_slice_in_dim(partial_value, (1 - parity) * half, half, 0)
    taken = partner(given, "col", 0)
    own_rows = lax.dynamic_slice_in_dim(partial_value, parity * half, half, 0)
    result = own_rows.astype(jnp.float32) + taken.astype(jnp.float32)
    return result.astype(jnp.bfloat16)[None, None]


def solution(mesh):
    in_specs = (
        P("col", "row", None, None, None),
        P("col", "row", None, None),
        P("col", "row", None, None),
        P("col", "row", None, None, None),
        P("col", "row", None, None),
        P("col", "row", None, None),
    )
    out_specs = P("col", "row", None, None, None)
    return jax.shard_map(
        on_device, mesh=mesh, in_specs=in_specs, out_specs=out_specs, check_vma=False
    )
```

profile of v0, /device:TPU:31, one launch (start us, length us, event | category | flops | bytes accessed | tf_op | source)
XLA Modules:
  0.0 1162.0 jit_solution(3729396354511272073)
XLA Ops:
  0.0 5.0 copy.76
  5.6 11.3 broadcast_in_dim.48
  16.8 836.0 %while.22 = (s32[]{:T(128)}, f32[16,512,1024]{2,1,0:T(8,128)}, bf16[16,32,128]{2,1,0:T(8,128)(2,1)S(1)}, f32[16,4]{1,0:T(8,128)S(1)}, f32[16,4]{1,0:T(8,128)S(1)...) while((s32[]{:T(128)}, f32[16,512,1024]{2,1,0:T(8,128)}, ...), condition=%wide.region_2.5_spmd, body=%wide.region_0.4_spmd.sunk | while | flops 17569472 | bytes 40623180 | solution.py:72
  16.8 4.9 copy.61
  23.2 4.1 collective-permute-start.4
  35.5 3.2 reshape.167
  38.8 3.3 multiply_bitcast_fusion.2
  44.7 3.7 reshape.168
  48.5 63.9 %collective-permute-done.2 = f32[16,4]{1,0:T(8,128)S(1)} collective-permute-done((f32[16,4]{1,0:T(8,128)S(1)}, f32[16,4]{1,0:T(8,128)S(1)}, u32[]{:S(2)}, u32[]{:S(2)}) %collective-permute-start.2) | collective-permute-done | bytes 288 | tf_op jit(solution)/shard_map/while/body/eval_jaxpr/ppermute | solution.py:11
  112.5 3.3 collective-permute-start.1
  115.8 36.7 %scatter_fusion = f32[16,512,1024]{2,1,0:T(8,128)} fusion(f32[16,512,1024]{2,1,0:T(8,128)} %get-tuple-element.161, s32[256]{0:T(256)S(1)} %reshape.165, f32[256,1024]{1,0:T(8,128)S(1)} %reshape.168), kind=kCustom, calls=%fused_computation.6.clone.1 | custom fusion | flops 262144 | bytes 3147776 | tf_op jit(solution)/shard_map/while/body/eval_jaxpr/scatter-add | solution.py:33
  152.5 4.9 copy.61
  157.4 4.0 collective-permute-start.3
  166.9 2.8 gather_fusion.1
  171.3 3.2 reshape.167
  174.6 3.3 multiply_bitcast_fusion.2
  180.5 3.7 reshape.168
  184.3 67.7 %collective-permute-done.2 = f32[16,4]{1,0:T(8,128)S(1)} collective-permute-done((f32[16,4]{1,0:T(8,128)S(1)}, f32[16,4]{1,0:T(8,128)S(1)}, u32[]{:S(2)}, u32[]{:S(2)}) %collective-permute-start.2) | collective-permute-done | bytes 288 | tf_op jit(solution)/shard_map/while/body/eval_jaxpr/ppermute | solution.py:11
  252.3 36.8 %scatter_fusion = f32[16,512,1024]{2,1,0:T(8,128)} fusion(f32[16,512,1024]{2,1,0:T(8,128)} %get-tuple-element.161, s32[256]{0:T(256)S(1)} %reshape.165, f32[256,1024]{1,0:T(8,128)S(1)} %reshape.168), kind=kCustom, calls=%fused_computation.6.clone.1 | custom fusion | flops 262144 | bytes 3147776 | tf_op jit(solution)/shard_map/while/body/eval_jaxpr/scatter-add | solution.py:33
  289.1 4.9 copy.61
  300.1 2.8 gather_fusion.1
  304.6 3.2 reshape.167
  307.9 3.3 multiply_bitcast_fusion.2
  313.7 3.7 reshape.168
  317.6 63.6 %collective-permute-done.2 = f32[16,4]{1,0:T(8,128)S(1)} collective-permute-done((f32[16,4]{1,0:T(8,128)S(1)}, f32[16,4]{1,0:T(8,128)S(1)}, u32[]{:S(2)}, u32[]{:S(2)}) %collective-permute-start.2) | collective-permute-done | bytes 288 | tf_op jit(solution)/shard_map/while/body/eval_jaxpr/ppermute | solution.py:11
  381.9 36.9 %scatter_fusion = f32[16,512,1024]{2,1,0:T(8,128)} fusion(f32[16,512,1024]{2,1,0:T(8,128)} %get-tuple-element.161, s32[256]{0:T(256)S(1)} %reshape.165, f32[256,1024]{1,0:T(8,128)S(1)} %reshape.168), kind=kCustom, calls=%fused_computation.6.clone.1 | custom fusion | flops 262144 | bytes 3147776 | tf_op jit(solution)/shard_map/while/body/eval_jaxpr/scatter-add | solution.py:33
  418.8 4.9 copy.61
  429.1 2.8 gather_fusion.1
  433.6 3.2 reshape.167
  436.8 3.3 multiply_bitcast_fusion.2
  442.7 3.7 reshape.168
  446.6 56.6 %collective-permute-done.2 = f32[16,4]{1,0:T(8,128)S(1)} collective-permute-done((f32[16,4]{1,0:T(8,128)S(1)}, f32[16,4]{1,0:T(8,128)S(1)}, u32[]{:S(2)}, u32[]{:S(2)}) %collective-permute-start.2) | collective-permute-done | bytes 288 | tf_op jit(solution)/shard_map/while/body/eval_jaxpr/ppermute | solution.py:11
  503.2 36.8 %scatter_fusion = f32[16,512,1024]{2,1,0:T(8,128)} fusion(f32[16,512,1024]{2,1,0:T(8,128)} %get-tuple-element.161, s32[256]{0:T(256)S(1)} %reshape.165, f32[256,1024]{1,0:T(8,128)S(1)} %reshape.168), kind=kCustom, calls=%fused_computation.6.clone.1 | custom fusion | flops 262144 | bytes 3147776 | tf_op jit(solution)/shard_map/while/body/eval_jaxpr/scatter-add | solution.py:33
  540.1 4.9 copy.61
  549.2 2.8 gather_fusion.1
  553.6 3.2 reshape.167
  556.9 3.3 multiply_bitcast_fusion.2
  562.8 3.7 reshape.168
  566.7 48.8 %collective-permute-done.2 = f32[16,4]{1,0:T(8,128)S(1)} collective-permute-done((f32[16,4]{1,0:T(8,128)S(1)}, f32[16,4]{1,0:T(8,128)S(1)}, u32[]{:S(2)}, u32[]{:S(2)}) %collective-permute-start.2) | collective-permute-done | bytes 288 | tf_op jit(solution)/shard_map/while/body/eval_jaxpr/ppermute | solution.py:11
  615.5 36.8 %scatter_fusion = f32[16,512,1024]{2,1,0:T(8,128)} fusion(f32[16,512,1024]{2,1,0:T(8,128)} %get-tuple-element.161, s32[256]{0:T(256)S(1)} %reshape.165, f32[256,1024]{1,0:T(8,128)S(1)} %reshape.168), kind=kCustom, calls=%fused_computation.6.clone.1 | custom fusion | flops 262144 | bytes 3147776 | tf_op jit(solution)/shard_map/while/body/eval_jaxpr/scatter-add | solution.py:33
  652.3 4.9 copy.61
  665.2 3.2 reshape.167
  668.5 3.3 multiply_bitcast_fusion.2
  674.4 3.7 reshape.168
  678.2 41.6 %collective-permute-done.2 = f32[16,4]{1,0:T(8,128)S(1)} collective-permute-done((f32[16,4]{1,0:T(8,128)S(1)}, f32[16,4]{1,0:T(8,128)S(1)}, u32[]{:S(2)}, u32[]{:S(2)}) %collective-permute-start.2) | collective-permute-done | bytes 288 | tf_op jit(solution)/shard_map/while/body/eval_jaxpr/ppermute | solution.py:11
  719.8 36.8 %scatter_fusion = f32[16,512,1024]{2,1,0:T(8,128)} fusion(f32[16,512,1024]{2,1,0:T(8,128)} %get-tuple-element.161, s32[256]{0:T(256)S(1)} %reshape.165, f32[256,1024]{1,0:T(8,128)S(1)} %reshape.168), kind=kCustom, calls=%fused_computation.6.clone.1 | custom fusion | flops 262144 | bytes 3147776 | tf_op jit(solution)/shard_map/while/body/eval_jaxpr/scatter-add | solution.py:33
  756.7 4.9 copy.61
  768.8 3.2 reshape.167
  772.1 3.3 multiply_bitcast_fusion.2
  778.0 3.7 reshape.168
  781.8 34.1 %collective-permute-done.2 = f32[16,4]{1,0:T(8,128)S(1)} collective-permute-done((f32[16,4]{1,0:T(8,128)S(1)}, f32[16,4]{1,0:T(8,128)S(1)}, u32[]{:S(2)}, u32[]{:S(2)}) %collective-permute-start.2) | collective-permute-done | bytes 288 | tf_op jit(solution)/shard_map/while/body/eval_jaxpr/ppermute | solution.py:11
  815.9 36.8 %scatter_fusion = f32[16,512,1024]{2,1,0:T(8,128)} fusion(f32[16,512,1024]{2,1,0:T(8,128)} %get-tuple-element.161, s32[256]{0:T(256)S(1)} %reshape.165, f32[256,1024]{1,0:T(8,128)S(1)} %reshape.168), kind=kCustom, calls=%fused_computation.6.clone.1 | custom fusion | flops 262144 | bytes 3147776 | tf_op jit(solution)/shard_map/while/body/eval_jaxpr/scatter-add | solution.py:33
  857.0 3.2 reshape.41
  860.3 4.8 fusion.11
  865.1 3.7 reshape.101
  869.7 37.0 %scatter_fusion.1 = f32[16,512,1024]{2,1,0:T(8,128)} fusion(f32[16,512,1024]{2,1,0:T(8,128)} %get-tuple-element.55, s32[256]{0:T(256)S(1)} %reshape.99, f32[256,1024]{1,0:T(8,128)S(1)} %reshape.101), kind=kCustom, calls=%fused_computation.7 | custom fusion | flops 262144 | bytes 3147776 | tf_op jit(solution)/shard_map/scatter-add | solution.py:33
  906.7 17.5 %convert_element_type.42 = bf16[16,512,1024]{2,1,0:T(8,128)(2,1)} convert(f32[16,512,1024]{2,1,0:T(8,128)} %scatter_fusion.1) | non-fusion elementwise | flops 8388608 | bytes 50331648 | tf_op jit(solution)/shard_map/convert_element_type | solution.py:76
  924.2 21.6 %copy.34 = bf16[16,512,1024]{1,2,0:T(8,128)(2,1)} copy(bf16[16,512,1024]{2,1,0:T(8,128)(2,1)} %convert_element_type.42) | data formatting | bytes 33554432 | tf_op jit(solution)/shard_map/optimization_barrier | solution.py:76
  945.8 53.9 %copy.35 = bf16[16,32,512,32]{3,2,1,0:T(8,128)(2,1)} copy(bf16[16,32,512,32]{2,3,1,0:T(8,128)(2,1)} %bitcast.59) | data formatting | bytes 33554432 | tf_op jit(solution)/shard_map/transpose | solution.py:78
  999.7 81.5 %reshape.44 = bf16[16,32,16384]{2,1,0:T(8,128)(2,1)} reshape(bf16[16,32,512,32]{3,2,1,0:T(8,128)(2,1)} %copy.35) | data formatting | bytes 33554432 | tf_op jit(solution)/shard_map/reshape | solution.py:78
  1081.2 7.7 constant_dynamic-slice_fusion
  1088.8 50.6 %collective-permute-start.6 = (bf16[8,32,16384]{2,1,0:T(8,128)(2,1)}, bf16[8,32,16384]{2,1,0:T(8,128)(2,1)}, u32[]{:S(2)}, u32[]{:S(2)}) collective-permute-start(bf16[8,32,16384]{2,1,0:T(8,128)(2,1)} %constant_dynamic-slice_fusion), channel_id=1, source_target_pairs={{0,1},{1,0},{2,3},{3,2},{4,5},{5,4},{6,7},{7,6},{8,9},{9,8},{10,11... | collective-permute-start | bytes 25165832 | tf_op jit(solution)/shard_map/ppermute | solution.py:17
  1139.4 13.1 %collective-permute-done.6 = bf16[8,32,16384]{2,1,0:T(8,128)(2,1)} collective-permute-done((bf16[8,32,16384]{2,1,0:T(8,128)(2,1)}, bf16[8,32,16384]{2,1,0:T(8,128)(2,1)}, u32[]{:S(2)}, u32[]{:S(2)}) %collective-permute-start.6) | collective-permute-done | bytes 8388640 | tf_op jit(solution)/shard_map/ppermute | solution.py:17
  1152.5 9.4 fusion.10
  (224 shorter events, 78.1 us)
Async XLA Ops:
  0.0 5.5 copy-start.3
  0.0 5.4 copy-start.4
  0.0 5.2 copy-start.2
  0.0 5.0 copy-start.1
  5.6 11.3 copy-start
  21.7 130.7 %collective-permute-start.3 = (bf16[512,32,128]{2,1,0:T(8,128)(2,1)}, bf16[512,32,128]{2,1,0:T(8,128)(2,1)}, u32[]{:S(2)}, u32[]{:S(2)}) collective-permute-start(bf16[512,32,128]{2,1,0:T(8,128)(2,1)} %copy.61), channel_id=1, source_target_pairs={{0,14},{1,15},{2,0},{3,1},{4,2},{5,3},{6,4},{7,5},{8,6},{9,7},{10,... | collective-permute-start | bytes 12582920 | tf_op jit(solution)/shard_map/while/body/eval_jaxpr/ppermute | solution.py:11
  22.3 90.2 %collective-permute-start.2 = (f32[16,4]{1,0:T(8,128)S(1)}, f32[16,4]{1,0:T(8,128)S(1)}, u32[]{:S(2)}, u32[]{:S(2)}) collective-permute-start(f32[16,4]{1,0:T(8,128)S(1)} %copy.60), channel_id=1, source_target_pairs={{0,112},{16,0},{32,16},{48,32},{64,48},{80,64},{96,80},{112,96},{1... | collective-permute-start | bytes 776 | tf_op jit(solution)/shard_map/while/body/eval_jaxpr/ppermute | solution.py:11
  23.2 129.3 %collective-permute-start.4 = (f32[512,4]{1,0:T(8,128)S(1)}, f32[512,4]{1,0:T(8,128)S(1)}, u32[]{:S(2)}, u32[]{:S(2)}) collective-permute-start(f32[512,4]{1,0:T(8,128)S(1)} %copy.62), channel_id=1, source_target_pairs={{0,14},{1,15},{2,0},{3,1},{4,2},{5,3},{6,4},{7,5},{8,6},{9,7},{10,... | collective-permute-start | bytes 24584 | tf_op jit(solution)/shard_map/while/body/eval_jaxpr/ppermute | solution.py:11
  27.3 125.1 %collective-permute-start.5 = (f32[512,4]{1,0:T(8,128)S(1)}, f32[512,4]{1,0:T(8,128)S(1)}, u32[]{:S(2)}, u32[]{:S(2)}) collective-permute-start(f32[512,4]{1,0:T(8,128)S(1)} %copy.63), channel_id=1, source_target_pairs={{0,14},{1,15},{2,0},{3,1},{4,2},{5,3},{6,4},{7,5},{8,6},{9,7},{10,... | collective-permute-start | bytes 24584 | tf_op jit(solution)/shard_map/while/body/eval_jaxpr/ppermute | solution.py:11
  28.3 124.2 %collective-permute-start = (bf16[16,32,128]{2,1,0:T(8,128)(2,1)S(1)}, bf16[16,32,128]{2,1,0:T(8,128)(2,1)S(1)}, u32[]{:S(2)}, u32[]{:S(2)}) collective-permute-start(bf16[16,32,128]{2,1,0:T(8,128)(2,1)S(1)} %copy.58), channel_id=1, source_target_pairs={{0,112},{16,0},{32,16},{48,32},{64,48},{80,64},{96,80},{112,96},{1... | collective-permute-start | bytes 393224 | tf_op jit(solution)/shard_map/while/body/eval_jaxpr/ppermute | solution.py:11
  112.5 40.0 %collective-permute-start.1 = (f32[16,4]{1,0:T(8,128)S(1)}, f32[16,4]{1,0:T(8,128)S(1)}, u32[]{:S(2)}, u32[]{:S(2)}) collective-permute-start(f32[16,4]{1,0:T(8,128)S(1)} %copy.59), channel_id=1, source_target_pairs={{0,112},{16,0},{32,16},{48,32},{64,48},{80,64},{96,80},{112,96},{1... | collective-permute-start | bytes 776 | tf_op jit(solution)/shard_map/while/body/eval_jaxpr/ppermute | solution.py:11
  157.4 131.7 %collective-permute-start.3 = (bf16[512,32,128]{2,1,0:T(8,128)(2,1)}, bf16[512,32,128]{2,1,0:T(8,128)(2,1)}, u32[]{:S(2)}, u32[]{:S(2)}) collective-permute-start(bf16[512,32,128]{2,1,0:T(8,128)(2,1)} %copy.61), channel_id=1, source_target_pairs={{0,14},{1,15},{2,0},{3,1},{4,2},{5,3},{6,4},{7,5},{8,6},{9,7},{10,... | collective-permute-start | bytes 12582920 | tf_op jit(solution)/shard_map/while/body/eval_jaxpr/ppermute | solution.py:11
  161.4 90.5 %collective-permute-start.2 = (f32[16,4]{1,0:T(8,128)S(1)}, f32[16,4]{1,0:T(8,128)S(1)}, u32[]{:S(2)}, u32[]{:S(2)}) collective-permute-start(f32[16,4]{1,0:T(8,128)S(1)} %copy.60), channel_id=1, source_target_pairs={{0,112},{16,0},{32,16},{48,32},{64,48},{80,64},{96,80},{112,96},{1... | collective-permute-start | bytes 776 | tf_op jit(solution)/shard_map/while/body/eval_jaxpr/ppermute | solution.py:11
  163.5 125.5 %collective-permute-start.4 = (f32[512,4]{1,0:T(8,128)S(1)}, f32[512,4]{1,0:T(8,128)S(1)}, u32[]{:S(2)}, u32[]{:S(2)}) collective-permute-start(f32[512,4]{1,0:T(8,128)S(1)} %copy.62), channel_id=1, source_target_pairs={{0,14},{1,15},{2,0},{3,1},{4,2},{5,3},{6,4},{7,5},{8,6},{9,7},{10,... | collective-permute-start | bytes 24584 | tf_op jit(solution)/shard_map/while/body/eval_jaxpr/ppermute | solution.py:11
  163.7 125.4 %collective-permute-start.5 = (f32[512,4]{1,0:T(8,128)S(1)}, f32[512,4]{1,0:T(8,128)S(1)}, u32[]{:S(2)}, u32[]{:S(2)}) collective-permute-start(f32[512,4]{1,0:T(8,128)S(1)} %copy.63), channel_id=1, source_target_pairs={{0,14},{1,15},{2,0},{3,1},{4,2},{5,3},{6,4},{7,5},{8,6},{9,7},{10,... | collective-permute-start | bytes 24584 | tf_op jit(solution)/shard_map/while/body/eval_jaxpr/ppermute | solution.py:11
  165.1 124.0 %collective-permute-start = (bf16[16,32,128]{2,1,0:T(8,128)(2,1)S(1)}, bf16[16,32,128]{2,1,0:T(8,128)(2,1)S(1)}, u32[]{:S(2)}, u32[]{:S(2)}) collective-permute-start(bf16[16,32,128]{2,1,0:T(8,128)(2,1)S(1)} %copy.58), channel_id=1, source_target_pairs={{0,112},{16,0},{32,16},{48,32},{64,48},{80,64},{96,80},{112,96},{1... | collective-permute-start | bytes 393224 | tf_op jit(solution)/shard_map/while/body/eval_jaxpr/ppermute | solution.py:11
  252.0 37.1 %collective-permute-start.1 = (f32[16,4]{1,0:T(8,128)S(1)}, f32[16,4]{1,0:T(8,128)S(1)}, u32[]{:S(2)}, u32[]{:S(2)}) collective-permute-start(f32[16,4]{1,0:T(8,128)S(1)} %copy.59), channel_id=1, source_target_pairs={{0,112},{16,0},{32,16},{48,32},{64,48},{80,64},{96,80},{112,96},{1... | collective-permute-start | bytes 776 | tf_op jit(solution)/shard_map/while/body/eval_jaxpr/ppermute | solution.py:11
  294.0 124.8 %collective-permute-start.3 = (bf16[512,32,128]{2,1,0:T(8,128)(2,1)}, bf16[512,32,128]{2,1,0:T(8,128)(2,1)}, u32[]{:S(2)}, u32[]{:S(2)}) collective-permute-start(bf16[512,32,128]{2,1,0:T(8,128)(2,1)} %copy.61), channel_id=1, source_target_pairs={{0,14},{1,15},{2,0},{3,1},{4,2},{5,3},{6,4},{7,5},{8,6},{9,7},{10,... | collective-permute-start | bytes 12582920 | tf_op jit(solution)/shard_map/while/body/eval_jaxpr/ppermute | solution.py:11
  295.3 85.9 %collective-permute-start.2 = (f32[16,4]{1,0:T(8,128)S(1)}, f32[16,4]{1,0:T(8,128)S(1)}, u32[]{:S(2)}, u32[]{:S(2)}) collective-permute-start(f32[16,4]{1,0:T(8,128)S(1)} %copy.60), channel_id=1, source_target_pairs={{0,112},{16,0},{32,16},{48,32},{64,48},{80,64},{96,80},{112,96},{1... | collective-permute-start | bytes 776 | tf_op jit(solution)/shard_map/while/body/eval_jaxpr/ppermute | solution.py:11
  296.9 121.9 %collective-permute-start.4 = (f32[512,4]{1,0:T(8,128)S(1)}, f32[512,4]{1,0:T(8,128)S(1)}, u32[]{:S(2)}, u32[]{:S(2)}) collective-permute-start(f32[512,4]{1,0:T(8,128)S(1)} %copy.62), channel_id=1, source_target_pairs={{0,14},{1,15},{2,0},{3,1},{4,2},{5,3},{6,4},{7,5},{8,6},{9,7},{10,... | collective-permute-start | bytes 24584 | tf_op jit(solution)/shard_map/while/body/eval_jaxpr/ppermute | solution.py:11
  297.6 121.2 %collective-permute-start.5 = (f32[512,4]{1,0:T(8,128)S(1)}, f32[512,4]{1,0:T(8,128)S(1)}, u32[]{:S(2)}, u32[]{:S(2)}) collective-permute-start(f32[512,4]{1,0:T(8,128)S(1)} %copy.63), channel_id=1, source_target_pairs={{0,14},{1,15},{2,0},{3,1},{4,2},{5,3},{6,4},{7,5},{8,6},{9,7},{10,... | collective-permute-start | bytes 24584 | tf_op jit(solution)/shard_map/while/body/eval_jaxpr/ppermute | solution.py:11
  298.3 120.5 %collective-permute-start = (bf16[16,32,128]{2,1,0:T(8,128)(2,1)S(1)}, bf16[16,32,128]{2,1,0:T(8,128)(2,1)S(1)}, u32[]{:S(2)}, u32[]{:S(2)}) collective-permute-start(bf16[16,32,128]{2,1,0:T(8,128)(2,1)S(1)} %copy.58), channel_id=1, source_target_pairs={{0,112},{16,0},{32,16},{48,32},{64,48},{80,64},{96,80},{112,96},{1... | collective-permute-start | bytes 393224 | tf_op jit(solution)/shard_map/while/body/eval_jaxpr/ppermute | solution.py:11
  381.2 37.6 %collective-permute-start.1 = (f32[16,4]{1,0:T(8,128)S(1)}, f32[16,4]{1,0:T(8,128)S(1)}, u32[]{:S(2)}, u32[]{:S(2)}) collective-permute-start(f32[16,4]{1,0:T(8,128)S(1)} %copy.59), channel_id=1, source_target_pairs={{0,112},{16,0},{32,16},{48,32},{64,48},{80,64},{96,80},{112,96},{1... | collective-permute-start | bytes 776 | tf_op jit(solution)/shard_map/while/body/eval_jaxpr/ppermute | solution.py:11
  423.7 116.4 %collective-permute-start.3 = (bf16[512,32,128]{2,1,0:T(8,128)(2,1)}, bf16[512,32,128]{2,1,0:T(8,128)(2,1)}, u32[]{:S(2)}, u32[]{:S(2)}) collective-permute-start(bf16[512,32,128]{2,1,0:T(8,128)(2,1)} %copy.61), channel_id=1, source_target_pairs={{0,14},{1,15},{2,0},{3,1},{4,2},{5,3},{6,4},{7,5},{8,6},{9,7},{10,... | collective-permute-start | bytes 12582920 | tf_op jit(solution)/shard_map/while/body/eval_jaxpr/ppermute | solution.py:11
  423.8 79.5 %collective-permute-start.2 = (f32[16,4]{1,0:T(8,128)S(1)}, f32[16,4]{1,0:T(8,128)S(1)}, u32[]{:S(2)}, u32[]{:S(2)}) collective-permute-start(f32[16,4]{1,0:T(8,128)S(1)} %copy.60), channel_id=1, source_target_pairs={{0,112},{16,0},{32,16},{48,32},{64,48},{80,64},{96,80},{112,96},{1... | collective-permute-start | bytes 776 | tf_op jit(solution)/shard_map/while/body/eval_jaxpr/ppermute | solution.py:11
  426.2 113.9 %collective-permute-start.4 = (f32[512,4]{1,0:T(8,128)S(1)}, f32[512,4]{1,0:T(8,128)S(1)}, u32[]{:S(2)}, u32[]{:S(2)}) collective-permute-start(f32[512,4]{1,0:T(8,128)S(1)} %copy.62), channel_id=1, source_target_pairs={{0,14},{1,15},{2,0},{3,1},{4,2},{5,3},{6,4},{7,5},{8,6},{9,7},{10,... | collective-permute-start | bytes 24584 | tf_op jit(solution)/shard_map/while/body/eval_jaxpr/ppermute | solution.py:11
  426.3 113.8 %collective-permute-start.5 = (f32[512,4]{1,0:T(8,128)S(1)}, f32[512,4]{1,0:T(8,128)S(1)}, u32[]{:S(2)}, u32[]{:S(2)}) collective-permute-start(f32[512,4]{1,0:T(8,128)S(1)} %copy.63), channel_id=1, source_target_pairs={{0,14},{1,15},{2,0},{3,1},{4,2},{5,3},{6,4},{7,5},{8,6},{9,7},{10,... | collective-permute-start | bytes 24584 | tf_op jit(solution)/shard_map/while/body/eval_jaxpr/ppermute | solution.py:11
  427.3 112.8 %collective-permute-start = (bf16[16,32,128]{2,1,0:T(8,128)(2,1)S(1)}, bf16[16,32,128]{2,1,0:T(8,128)(2,1)S(1)}, u32[]{:S(2)}, u32[]{:S(2)}) collective-permute-start(bf16[16,32,128]{2,1,0:T(8,128)(2,1)S(1)} %copy.58), channel_id=1, source_target_pairs={{0,112},{16,0},{32,16},{48,32},{64,48},{80,64},{96,80},{112,96},{1... | collective-permute-start | bytes 393224 | tf_op jit(solution)/shard_map/while/body/eval_jaxpr/ppermute | solution.py:11
  503.2 36.9 %collective-permute-start.1 = (f32[16,4]{1,0:T(8,128)S(1)}, f32[16,4]{1,0:T(8,128)S(1)}, u32[]{:S(2)}, u32[]{:S(2)}) collective-permute-start(f32[16,4]{1,0:T(8,128)S(1)} %copy.59), channel_id=1, source_target_pairs={{0,112},{16,0},{32,16},{48,32},{64,48},{80,64},{96,80},{112,96},{1... | collective-permute-start | bytes 776 | tf_op jit(solution)/shard_map/while/body/eval_jaxpr/ppermute | solution.py:11
  545.0 107.2 %collective-permute-start.3 = (bf16[512,32,128]{2,1,0:T(8,128)(2,1)}, bf16[512,32,128]{2,1,0:T(8,128)(2,1)}, u32[]{:S(2)}, u32[]{:S(2)}) collective-permute-start(bf16[512,32,128]{2,1,0:T(8,128)(2,1)} %copy.61), channel_id=1, source_target_pairs={{0,14},{1,15},{2,0},{3,1},{4,2},{5,3},{6,4},{7,5},{8,6},{9,7},{10,... | collective-permute-start | bytes 12582920 | tf_op jit(solution)/shard_map/while/body/eval_jaxpr/ppermute | solution.py:11
  545.1 70.4 %collective-permute-start.2 = (f32[16,4]{1,0:T(8,128)S(1)}, f32[16,4]{1,0:T(8,128)S(1)}, u32[]{:S(2)}, u32[]{:S(2)}) collective-permute-start(f32[16,4]{1,0:T(8,128)S(1)} %copy.60), channel_id=1, source_target_pairs={{0,112},{16,0},{32,16},{48,32},{64,48},{80,64},{96,80},{112,96},{1... | collective-permute-start | bytes 776 | tf_op jit(solution)/shard_map/while/body/eval_jaxpr/ppermute | solution.py:11
  545.8 106.5 %collective-permute-start.4 = (f32[512,4]{1,0:T(8,128)S(1)}, f32[512,4]{1,0:T(8,128)S(1)}, u32[]{:S(2)}, u32[]{:S(2)}) collective-permute-start(f32[512,4]{1,0:T(8,128)S(1)} %copy.62), channel_id=1, source_target_pairs={{0,14},{1,15},{2,0},{3,1},{4,2},{5,3},{6,4},{7,5},{8,6},{9,7},{10,... | collective-permute-start | bytes 24584 | tf_op jit(solution)/shard_map/while/body/eval_jaxpr/ppermute | solution.py:11
  546.2 106.1 %collective-permute-start.5 = (f32[512,4]{1,0:T(8,128)S(1)}, f32[512,4]{1,0:T(8,128)S(1)}, u32[]{:S(2)}, u32[]{:S(2)}) collective-permute-start(f32[512,4]{1,0:T(8,128)S(1)} %copy.63), channel_id=1, source_target_pairs={{0,14},{1,15},{2,0},{3,1},{4,2},{5,3},{6,4},{7,5},{8,6},{9,7},{10,... | collective-permute-start | bytes 24584 | tf_op jit(solution)/shard_map/while/body/eval_jaxpr/ppermute | solution.py:11
  547.2 105.0 %collective-permute-start = (bf16[16,32,128]{2,1,0:T(8,128)(2,1)S(1)}, bf16[16,32,128]{2,1,0:T(8,128)(2,1)S(1)}, u32[]{:S(2)}, u32[]{:S(2)}) collective-permute-start(bf16[16,32,128]{2,1,0:T(8,128)(2,1)S(1)} %copy.58), channel_id=1, source_target_pairs={{0,112},{16,0},{32,16},{48,32},{64,48},{80,64},{96,80},{112,96},{1... | collective-permute-start | bytes 393224 | tf_op jit(solution)/shard_map/while/body/eval_jaxpr/ppermute | solution.py:11
  615.5 36.8 %collective-permute-start.1 = (f32[16,4]{1,0:T(8,128)S(1)}, f32[16,4]{1,0:T(8,128)S(1)}, u32[]{:S(2)}, u32[]{:S(2)}) collective-permute-start(f32[16,4]{1,0:T(8,128)S(1)} %copy.59), channel_id=1, source_target_pairs={{0,112},{16,0},{32,16},{48,32},{64,48},{80,64},{96,80},{112,96},{1... | collective-permute-start | bytes 776 | tf_op jit(solution)/shard_map/while/body/eval_jaxpr/ppermute | solution.py:11
  657.2 99.4 %collective-permute-start.3 = (bf16[512,32,128]{2,1,0:T(8,128)(2,1)}, bf16[512,32,128]{2,1,0:T(8,128)(2,1)}, u32[]{:S(2)}, u32[]{:S(2)}) collective-permute-start(bf16[512,32,128]{2,1,0:T(8,128)(2,1)} %copy.61), channel_id=1, source_target_pairs={{0,14},{1,15},{2,0},{3,1},{4,2},{5,3},{6,4},{7,5},{8,6},{9,7},{10,... | collective-permute-start | bytes 12582920 | tf_op jit(solution)/shard_map/while/body/eval_jaxpr/ppermute | solution.py:11
  657.5 62.3 %collective-permute-start.2 = (f32[16,4]{1,0:T(8,128)S(1)}, f32[16,4]{1,0:T(8,128)S(1)}, u32[]{:S(2)}, u32[]{:S(2)}) collective-permute-start(f32[16,4]{1,0:T(8,128)S(1)} %copy.60), channel_id=1, source_target_pairs={{0,112},{16,0},{32,16},{48,32},{64,48},{80,64},{96,80},{112,96},{1... | collective-permute-start | bytes 776 | tf_op jit(solution)/shard_map/while/body/eval_jaxpr/ppermute | solution.py:11
  657.6 99.0 %collective-permute-start.4 = (f32[512,4]{1,0:T(8,128)S(1)}, f32[512,4]{1,0:T(8,128)S(1)}, u32[]{:S(2)}, u32[]{:S(2)}) collective-permute-start(f32[512,4]{1,0:T(8,128)S(1)} %copy.62), channel_id=1, source_target_pairs={{0,14},{1,15},{2,0},{3,1},{4,2},{5,3},{6,4},{7,5},{8,6},{9,7},{10,... | collective-permute-start | bytes 24584 | tf_op jit(solution)/shard_map/while/body/eval_jaxpr/ppermute | solution.py:11
  658.7 98.0 %collective-permute-start.5 = (f32[512,4]{1,0:T(8,128)S(1)}, f32[512,4]{1,0:T(8,128)S(1)}, u32[]{:S(2)}, u32[]{:S(2)}) collective-permute-start(f32[512,4]{1,0:T(8,128)S(1)} %copy.63), channel_id=1, source_target_pairs={{0,14},{1,15},{2,0},{3,1},{4,2},{5,3},{6,4},{7,5},{8,6},{9,7},{10,... | collective-permute-start | bytes 24584 | tf_op jit(solution)/shard_map/while/body/eval_jaxpr/ppermute | solution.py:11
  659.2 97.4 %collective-permute-start = (bf16[16,32,128]{2,1,0:T(8,128)(2,1)S(1)}, bf16[16,32,128]{2,1,0:T(8,128)(2,1)S(1)}, u32[]{:S(2)}, u32[]{:S(2)}) collective-permute-start(bf16[16,32,128]{2,1,0:T(8,128)(2,1)S(1)} %copy.58), channel_id=1, source_target_pairs={{0,112},{16,0},{32,16},{48,32},{64,48},{80,64},{96,80},{112,96},{1... | collective-permute-start | bytes 393224 | tf_op jit(solution)/shard_map/while/body/eval_jaxpr/ppermute | solution.py:11
  719.8 36.8 %collective-permute-start.1 = (f32[16,4]{1,0:T(8,128)S(1)}, f32[16,4]{1,0:T(8,128)S(1)}, u32[]{:S(2)}, u32[]{:S(2)}) collective-permute-start(f32[16,4]{1,0:T(8,128)S(1)} %copy.59), channel_id=1, source_target_pairs={{0,112},{16,0},{32,16},{48,32},{64,48},{80,64},{96,80},{112,96},{1... | collective-permute-start | bytes 776 | tf_op jit(solution)/shard_map/while/body/eval_jaxpr/ppermute | solution.py:11
  761.6 91.2 %collective-permute-start.3 = (bf16[512,32,128]{2,1,0:T(8,128)(2,1)}, bf16[512,32,128]{2,1,0:T(8,128)(2,1)}, u32[]{:S(2)}, u32[]{:S(2)}) collective-permute-start(bf16[512,32,128]{2,1,0:T(8,128)(2,1)} %copy.61), channel_id=1, source_target_pairs={{0,14},{1,15},{2,0},{3,1},{4,2},{5,3},{6,4},{7,5},{8,6},{9,7},{10,... | collective-permute-start | bytes 12582920 | tf_op jit(solution)/shard_map/while/body/eval_jaxpr/ppermute | solution.py:11
  761.6 54.3 %collective-permute-start.2 = (f32[16,4]{1,0:T(8,128)S(1)}, f32[16,4]{1,0:T(8,128)S(1)}, u32[]{:S(2)}, u32[]{:S(2)}) collective-permute-start(f32[16,4]{1,0:T(8,128)S(1)} %copy.60), channel_id=1, source_target_pairs={{0,112},{16,0},{32,16},{48,32},{64,48},{80,64},{96,80},{112,96},{1... | collective-permute-start | bytes 776 | tf_op jit(solution)/shard_map/while/body/eval_jaxpr/ppermute | solution.py:11
  761.6 91.2 %collective-permute-start.4 = (f32[512,4]{1,0:T(8,128)S(1)}, f32[512,4]{1,0:T(8,128)S(1)}, u32[]{:S(2)}, u32[]{:S(2)}) collective-permute-start(f32[512,4]{1,0:T(8,128)S(1)} %copy.62), channel_id=1, source_target_pairs={{0,14},{1,15},{2,0},{3,1},{4,2},{5,3},{6,4},{7,5},{8,6},{9,7},{10,... | collective-permute-start | bytes 24584 | tf_op jit(solution)/shard_map/while/body/eval_jaxpr/ppermute | solution.py:11
  763.6 89.2 %collective-permute-start.5 = (f32[512,4]{1,0:T(8,128)S(1)}, f32[512,4]{1,0:T(8,128)S(1)}, u32[]{:S(2)}, u32[]{:S(2)}) collective-permute-start(f32[512,4]{1,0:T(8,128)S(1)} %copy.63), channel_id=1, source_target_pairs={{0,14},{1,15},{2,0},{3,1},{4,2},{5,3},{6,4},{7,5},{8,6},{9,7},{10,... | collective-permute-start | bytes 24584 | tf_op jit(solution)/shard_map/while/body/eval_jaxpr/ppermute | solution.py:11
  763.7 89.1 %collective-permute-start = (bf16[16,32,128]{2,1,0:T(8,128)(2,1)S(1)}, bf16[16,32,128]{2,1,0:T(8,128)(2,1)S(1)}, u32[]{:S(2)}, u32[]{:S(2)}) collective-permute-start(bf16[16,32,128]{2,1,0:T(8,128)(2,1)S(1)} %copy.58), channel_id=1, source_target_pairs={{0,112},{16,0},{32,16},{48,32},{64,48},{80,64},{96,80},{112,96},{1... | collective-permute-start | bytes 393224 | tf_op jit(solution)/shard_map/while/body/eval_jaxpr/ppermute | solution.py:11
  815.9 36.9 %collective-permute-start.1 = (f32[16,4]{1,0:T(8,128)S(1)}, f32[16,4]{1,0:T(8,128)S(1)}, u32[]{:S(2)}, u32[]{:S(2)}) collective-permute-start(f32[16,4]{1,0:T(8,128)S(1)} %copy.59), channel_id=1, source_target_pairs={{0,112},{16,0},{32,16},{48,32},{64,48},{80,64},{96,80},{112,96},{1... | collective-permute-start | bytes 776 | tf_op jit(solution)/shard_map/while/body/eval_jaxpr/ppermute | solution.py:11
  1088.8 63.7 %collective-permute-start.6 = (bf16[8,32,16384]{2,1,0:T(8,128)(2,1)}, bf16[8,32,16384]{2,1,0:T(8,128)(2,1)}, u32[]{:S(2)}, u32[]{:S(2)}) collective-permute-start(bf16[8,32,16384]{2,1,0:T(8,128)(2,1)} %constant_dynamic-slice_fusion), channel_id=1, source_target_pairs={{0,1},{1,0},{2,3},{3,2},{4,5},{5,4},{6,7},{7,6},{8,9},{9,8},{10,11... | collective-permute-start | bytes 25165832 | tf_op jit(solution)/shard_map/ppermute | solution.py:17
where the time goes:
time: 1180 us; the launch traced here: 1160 us
  waiting for transfers between devices  390 us (33%)
  other arithmetic  351 us (30%)
  local copies, waits for them, and re-layouts  325 us (28%)
  starting transfers between devices  92.7 us (8%)
    ppermute x42, waiting for transfers between devices, from_behind(): lax.ppermute(shard, axis, [(i, (i + by) % devices) for i in range(devices)])  376 us
    scatter-add x8, other arithmetic, block_sum(): return total.at[row_ids, right_idx].add(scaled)  295 us
    reshape x1, local copies, waits for them, and re-layouts, on_device(): jnp.transpose(rounded, (0, 2, 1, 3)).reshape(nrows, bsize, JW * bsize)  81.5 us
    transpose x1, local copies, waits for them, and re-layouts, on_device(): jnp.transpose(rounded, (0, 2, 1, 3)).reshape(nrows, bsize, JW * bsize)  53.9 us
    ppermute x1, starting transfers between devices, partner(): return lax.ppermute(value, axis, pairs)  50.6 us
    ppermute x42, starting transfers between devices, from_behind(): lax.ppermute(shard, axis, [(i, (i + by) % devices) for i in range(devices)])  42.1 us
    another operation x42, local copies, waits for them, and re-layouts  34.8 us
    reshape x8, local copies, waits for them, and re-layouts, block_sum(): scaled = scaled.reshape(nrows, slots_a, slots_b, bsize * bsize)  30 us
  transfers between devices with their start and end apart: 43, of which 8 were waited for; matrix products, arithmetic and copies ran while one was open for 33% of the time, Pallas kernels for 0%

commit v1 on v0

v1 whole, which is shorter than its diff:
```python
import jax
import jax.numpy as jnp
from jax import lax
from jax.experimental import pallas as pl
from jax.experimental.pallas import tpu as pltpu
from jax.sharding import PartitionSpec as P

MESH = pl.DeviceIdType.MESH
F32, BF16, I32 = jnp.float32, jnp.bfloat16, jnp.int32

OFFSETS = ((1, 0), (0, 1), (3, 0), (1, 1), (2, 0), (3, 1), (2, 1), (0, 0))
HOPS = (1, 3, 2)


def lane_groups(v, group):
    low, high = group % 2 == 0, group < 2
    t = [None] * 4
    for i in (0, 2):
        t[i] = jnp.where(low, v[i], pltpu.roll(v[i + 1], 32, 1))
        t[i + 1] = jnp.where(low, pltpu.roll(v[i], 96, 1), v[i + 1])
    w = [None] * 4
    for i in (0, 1):
        w[i] = jnp.where(high, t[i], pltpu.roll(t[i + 2], 64, 1))
        w[i + 2] = jnp.where(high, pltpu.roll(t[i], 64, 1), t[i + 2])
    return w


def exchange_kernel(
    cols_ref, scale_ref, a_ref, b_ref, bs_ref, bc_ref,
    brecv, arecv, ocols, oscale,
    b_vm, bsend, idx_s, idx_r, as_s, as_r, idx_sm, as_sm, table, msend, mrecv,
    local_sem, idx_ss, idx_rs, as_ss, as_rs, b_ss, b_rs, m_ss, m_rs, a_ss, a_rs,
):
    c, r = lax.axis_index("col"), lax.axis_index("row")
    s, q = c // 2, c % 2
    z, xl, y, xh = s // 2, s % 2, r // 2, r % 2
    k = (s + r) % 8
    rx = y * 2 + (1 - xh)
    kx = (s + rx) % 8

    def dev(s_, q_, r_):
        return {"row": r_, "col": 2 * s_ + q_}

    def chip(d):
        dz, dx = OFFSETS[d]
        return ((z + dz) % 4) * 2 + (1 - xl if dx else xl)

    def chip_behind(d):
        dz, dx = OFFSETS[d]
        return ((z + 4 - dz) % 4) * 2 + (1 - xl if dx else xl)

    def row_at(dy):
        return ((y + dy) % 4) * 2 + xh

    def send(src, dst, ssem, rsem, target):
        return pltpu.make_async_remote_copy(
            src_ref=src, dst_ref=dst, send_sem=ssem, recv_sem=rsem, device_id=target, device_id_type=MESH
        )

    load_b = pltpu.make_async_copy(b_ref, b_vm, local_sem.at[0])
    load_b.start()
    idx_s[...] = jnp.zeros_like(idx_s)
    as_s[...] = jnp.zeros_like(as_s)
    idx_s[0:4, 0:16] = cols_ref[...]
    as_s[0:4, 0:16] = scale_ref[...]

    barrier = pltpu.get_barrier_semaphore()
    peers = []
    for d in range(8):
        for p in range(2):
            if d < 7:
                peers.append(dev(chip(d), p, r))
    peers.append(dev(s, 1 - q, r))
    for p in range(2):
        peers.append(dev(s, p, rx))
    for dy in HOPS:
        peers.append(dev(s, q, row_at(dy)))
    for e in range(1, 8):
        peers.append(dev((s + 8 - e) % 8, q, (r + e) % 8))
    for peer in peers:
        pl.semaphore_signal(barrier, inc=1, device_id=peer, device_id_type=MESH)
    pl.semaphore_wait(barrier, len(peers))

    idx_sends = []
    for e in range(1, 8):
        to = dev((s + 8 - e) % 8, q, (r + e) % 8)
        idx_sends.append(send(idx_s, idx_r.at[s], idx_ss.at[e - 1], idx_rs.at[s], to))
        idx_sends.append(send(as_s, as_r.at[s], as_ss.at[e - 1], as_rs.at[s], to))
    for copy in idx_sends:
        copy.start()

    own_half = a_ref.at[pl.ds(pl.multiple_of(q * 8, 8), 8)]
    other_half = a_ref.at[pl.ds(pl.multiple_of((1 - q) * 8, 8), 8)]
    a_sends = [send(a_ref.at[pl.ds(p * 8, 8)], arecv.at[k, q], a_ss.at[1 + p], a_rs.at[1 + q], dev(s, p, rx)) for p in range(2)]
    a_sends.append(send(other_half, arecv.at[k, q], a_ss.at[0], a_rs.at[0], dev(s, 1 - q, r)))
    for copy in a_sends:
        copy.start()
    own_a = pltpu.make_async_copy(own_half, arecv.at[k, q], local_sem.at[1])
    own_a.start()

    idx_r[s] = idx_s[...]
    as_r[s] = as_s[...]
    for g in range(4):
        lanes = pl.ds(g * 128, 128)
        eight = jnp.concatenate([bs_ref[:, lanes], bc_ref[:, lanes].astype(F32)], axis=0)
        table[pl.ds(g * 128, 128), :] = jnp.transpose(jnp.concatenate([eight] * 16, axis=0))

    for e in range(1, 8):
        sb, rb = (s + e) % 8, (r + 8 - e) % 8
        send(idx_s, idx_r.at[sb], idx_ss.at[e - 1], idx_rs.at[sb], dev(sb, q, rb)).wait_recv()
        send(as_s, as_r.at[sb], as_ss.at[e - 1], as_rs.at[sb], dev(sb, q, rb)).wait_recv()
    to_smem = pltpu.make_async_copy(idx_r, idx_sm, local_sem.at[2])
    to_smem.start()
    to_smem2 = pltpu.make_async_copy(as_r, as_sm, local_sem.at[3])
    to_smem2.start()
    to_smem.wait()
    to_smem2.wait()
    load_b.wait()

    b_sends = []
    pending = []
    for d in range(8):
        sd = chip(d)

        def gather(i, _):
            for m in range(4):
                bsend[d, i // 8, (i % 8) * 4 + m] = b_vm[idx_sm[sd, m, i]]
            return _

        lax.fori_loop(0, 16, gather, 0)
        for copy in pending:
            copy.start()
        b_sends += pending
        pending = []
        if d < 7:
            for p in range(2):
                pending.append(send(bsend.at[d, p], brecv.at[k, q], b_ss.at[2 * d + p], b_rs.at[k, q], dev(sd, p, r)))
    own_b = pltpu.make_async_copy(bsend.at[7, q], brecv.at[k, q], local_sem.at[4])
    to_core = send(bsend.at[7, 1 - q], brecv.at[k, q], b_ss.at[14], b_rs.at[k, q], dev(s, 1 - q, r))

    own_a.wait()
    send(other_half, arecv.at[k, 1 - q], a_ss.at[0], a_rs.at[0], dev(s, 1 - q, r)).wait_recv()
    for p in range(2):
        send(own_half, arecv.at[kx, p], a_ss.at[1 + p], a_rs.at[1 + p], dev(s, p, rx)).wait_recv()
    own_b.start()
    to_core.start()
    for h, dy in enumerate(HOPS):
        for j, slot in enumerate((k, kx)):
            n = 3 + 2 * h + j
            copy = send(arecv.at[slot], arecv.at[slot], a_ss.at[n], a_rs.at[n], dev(s, q, row_at(dy)))
            copy.start()
            a_sends.append(copy)

    lane = lax.broadcasted_iota(I32, (1, 128), 1)
    part, place = lane % 8, lane // 8
    m_sends = []
    for d in range(8):
        sd = chip(d)

        def metas(n, _):
            row = jnp.zeros((1, 128), F32)
            for w in range(16):
                i, m = n * 4 + w // 4, w % 4
                factor = jnp.where(part < 4, as_sm[sd, m, i], 1.0)
                row = jnp.where(place == w, table[pl.ds(idx_sm[sd, m, i], 1), :] * factor, row)
            msend[d, n // 2, pl.ds(n % 2, 1), :] = row
            return _

        lax.fori_loop(0, 4, metas, 0)
    for d in range(7):
        for p in range(2):
            copy = send(msend.at[d, p], mrecv.at[k, q], m_ss.at[2 * d + p], m_rs.at[k, q], dev(chip(d), p, r))
            copy.start()
            m_sends.append(copy)
    copy = send(msend.at[7, 1 - q], mrecv.at[k, q], m_ss.at[14], m_rs.at[k, q], dev(s, 1 - q, r))
    copy.start()
    m_sends.append(copy)
    mrecv[k, q] = msend[7, q]

    own_b.wait()
    for d in range(8):
        sb = chip_behind(d)
        kb = (sb + r) % 8
        for p in range(2):
            if d < 7:
                send(bsend.at[d, p], brecv.at[kb, p], b_ss.at[2 * d + p], b_rs.at[kb, p], dev(sb, p, r)).wait_recv()
                send(msend.at[d, p], mrecv.at[kb, p], m_ss.at[2 * d + p], m_rs.at[kb, p], dev(sb, p, r)).wait_recv()
    send(bsend.at[7, q], brecv.at[k, 1 - q], b_ss.at[14], b_rs.at[k, 1 - q], dev(s, 1 - q, r)).wait_recv()
    send(msend.at[7, q], mrecv.at[k, 1 - q], m_ss.at[14], m_rs.at[k, 1 - q], dev(s, 1 - q, r)).wait_recv()
    for h, dy in enumerate(HOPS):
        rb = row_at(4 - dy)
        for j, rr in enumerate((rb, (rb // 2) * 2 + (1 - xh))):
            slot = (s + rr) % 8
            n = 3 + 2 * h + j
            send(arecv.at[slot], arecv.at[slot], a_ss.at[n], a_rs.at[n], dev(s, q, rb)).wait_recv()
    for kk in range(8):
        for qq in range(2):
            two = mrecv[kk, qq, 0:2, :]
            n = (kk * 2 + qq) * 2
            ocols[n:n + 2, :] = two.astype(I32)
            oscale[n:n + 2, :] = two
    for copy in idx_sends + a_sends + b_sends + [to_core] + m_sends:
        copy.wait_send()


def product_kernel(cols, scale, a_ref, b_ref, out_ref, x_ref, *accs):
    g = pl.program_id(0)
    group = lax.broadcasted_iota(I32, (8, 128), 1) // 32
    half = lax.broadcasted_iota(I32, (32, 128), 1) // 32

    @pl.when(g == 0)
    def _():
        def clear(t, _):
            for acc in accs:
                acc[pl.ds(t * 8, 8)] = jnp.zeros((8, 8, 128), F32)
            return _

        lax.fori_loop(0, 64, clear, 0)

    @pl.when(g < 16)
    def _():
        def products(i, _):
            a = a_ref[0, 0, i]
            zero = jnp.zeros_like(a)
            left = jnp.concatenate([jnp.where(half == m, a, zero) for m in range(4)], axis=0)
            right = b_ref[0, 0, pl.ds(i * 4, 4)].reshape(128, 128)
            prod = jnp.dot(left, right, preferred_element_type=F32)
            for m in range(4):
                rows = [prod[m * 32 + h * 8:m * 32 + h * 8 + 8, :] for h in range(4)]
                for n, block in enumerate(lane_groups(rows, group)):
                    x_ref[i, m * 4 + n] = block
            return _

        lax.fori_loop(0, 8, products, 0)

        def scatter(w, _):
            m, n = w // 4, w % 4
            for i, acc in enumerate(accs):
                row, lane = 2 * g + i // 4, ((i % 4) * 4 + m) * 8 + n
                j = cols[row, lane + 4]
                acc[j] = acc[j] + x_ref[i, w] * scale[row, lane]
            return _

        lax.fori_loop(0, 16, scatter, 0)

    for i, acc in enumerate(accs):
        @pl.when(g == 16 + i)
        def _(acc=acc):
            def tile(jt, _):
                w = lane_groups([acc[jt * 4 + n] for n in range(4)], group)
                lanes = pl.ds(pl.multiple_of(jt * 128, 128), 128)
                out_ref[0, :, lanes] = jnp.concatenate(w, axis=0).astype(BF16)
                return _

            lax.fori_loop(0, 128, tile, 0)


def on_device(a_blocks, a_scale, a_cols, b_blocks, b_scale, b_cols):
    vmem = pl.BlockSpec(memory_space=pltpu.VMEM)
    hbm = pl.BlockSpec(memory_space=pl.ANY)
    dma = pltpu.SemaphoreType.DMA
    brecv, arecv, cols, scale = pl.pallas_call(
        exchange_kernel,
        name="exchange",
        out_shape=(
            jax.ShapeDtypeStruct((8, 2, 32, 32, 128), BF16),
            jax.ShapeDtypeStruct((8, 2, 8, 32, 128), BF16),
            jax.ShapeDtypeStruct((32, 128), I32),
            jax.ShapeDtypeStruct((32, 128), F32),
        ),
        in_specs=[vmem, vmem, vmem, hbm, vmem, vmem],
        out_specs=(hbm, hbm, vmem, vmem),
        scratch_shapes=[
            pltpu.VMEM((512, 32, 128), BF16),
            pltpu.VMEM((8, 2, 32, 32, 128), BF16),
            pltpu.VMEM((8, 128), I32),
            pltpu.VMEM((8, 8, 128), I32),
            pltpu.VMEM((8, 128), F32),
            pltpu.VMEM((8, 8, 128), F32),
            pltpu.SMEM((8, 8, 128), I32),
            pltpu.SMEM((8, 8, 128), F32),
            pltpu.VMEM((512, 128), F32),
            pltpu.VMEM((8, 2, 8, 128), F32),
            pltpu.VMEM((8, 2, 8, 128), F32),
            dma((5,)), dma((7,)), dma((8,)), dma((7,)), dma((8,)),
            dma((15,)), dma((8, 2)), dma((15,)), dma((8, 2)), dma((9,)), dma((9,)),
        ],
        compiler_params=pltpu.CompilerParams(collective_id=0, has_side_effects=True, vmem_limit_bytes=32 << 20),
    )(a_cols[0, 0].T, a_scale[0, 0].T, a_blocks[0, 0], b_blocks[0, 0], b_scale[0, 0].T, b_cols[0, 0].T)
    out = pl.pallas_call(
        product_kernel,
        name="products",
        grid=(24,),
        out_shape=jax.ShapeDtypeStruct((8, 32, 16384), BF16),
        in_specs=[
            pl.BlockSpec(memory_space=pltpu.SMEM),
            pl.BlockSpec(memory_space=pltpu.SMEM),
            pl.BlockSpec((1, 1, 8, 32, 128), lambda g: (jnp.minimum(g, 15) // 2, jnp.minimum(g, 15) % 2, 0, 0, 0)),
            pl.BlockSpec((1, 1, 32, 32, 128), lambda g: (jnp.minimum(g, 15) // 2, jnp.minimum(g, 15) % 2, 0, 0, 0)),
        ],
        out_specs=pl.BlockSpec((1, 32, 16384), lambda g: (jnp.maximum(g - 16, 0), 0, 0)),
        scratch_shapes=[pltpu.VMEM((8, 16, 8, 128), F32)] + [pltpu.VMEM((512, 8, 128), F32)] * 8,
        compiler_params=pltpu.CompilerParams(vmem_limit_bytes=32 << 20),
    )(cols, scale, arecv, brecv)
    return out[None, None]


def solution(mesh):
    blocks = P("col", "row", None, None, None)
    small = P("col", "row", None, None)
    return jax.shard_map(
        on_device,
        mesh=mesh,
        in_specs=(blocks, small, small, blocks, small, small),
        out_specs=blocks,
        check_vma=False,
    )
```

time: 1180 us -> 278 us (0.24); the launches traced: 1160 us -> 276 us
  waiting for transfers between devices: 390 us -> 0 us
  other arithmetic: 351 us -> 0 us
  local copies, waits for them, and re-layouts: 325 us -> 5.85 us
  Pallas kernels: 0 us -> 270 us
  starting transfers between devices: 92.7 us -> 0 us
    ppermute x43 -> x0, waiting for transfers between devices: 390 us -> none  [the longest x42 376 us: from_behind(): lax.ppermute(shard, axis, [(i, (i + by) % devices) for i in range(devices)])]
    scatter-add x8 -> x0, other arithmetic: 295 us -> none  [block_sum(): return total.at[row_ids, right_idx].add(scaled)]
    pallas_call x0 -> x2, Pallas kernels: none -> 270 us  [the longest x1 203 us: on_device(): pl.pallas_call(product_kernel, name='products', grid=(24,), out_shape=jax...]
    reshape x25 -> x0, local copies, waits for them, and re-layouts: 139 us -> none  [the longest x1 81.5 us: on_device(): jnp.transpose(rounded, (0, 2, 1, 3)).reshape(nrows, bsize, JW * bsize)]
    ppermute x43 -> x0, starting transfers between devices: 92.7 us -> none  [the longest x1 50.6 us: partner(): return lax.ppermute(value, axis, pairs)]
    transpose x1 -> x0, local copies, waits for them, and re-layouts: 53.9 us -> none  [on_device(): jnp.transpose(rounded, (0, 2, 1, 3)).reshape(nrows, bsize, JW * bsize)]
    another operation x42 -> x0, local copies, waits for them, and re-layouts: 34.8 us -> none
    gather x24 -> x0, local copies, waits for them, and re-layouts: 32.3 us -> none  [the longest x8 22.8 us: apply_state(): rows = jnp.take(held, a_idx, axis=0)]
  transfers between devices with their start and end apart: 43 -> 0, of which waited for: 8 -> 0; matrix products, arithmetic and copies ran while one was open for 33% -> 0% of each run, Pallas kernels for 0% -> 0%
where the time goes in v1:
time: 278 us; the launch traced here: 276 us
  Pallas kernels  270 us (97%)
  local copies, waits for them, and re-layouts  5.85 us (2%)
    pallas_call x1, Pallas kernels, on_device(): pl.pallas_call(product_kernel, name='products', grid=(24,), out_shape=jax...  203 us
    pallas_call x1, Pallas kernels, on_device(): pl.pallas_call(exchange_kernel, name='exchange', out_shape=(jax.ShapeDtyp...  67.8 us
    unnamed x12, local copies, waits for them, and re-layouts  5.85 us

profile of v1, /device:TPU:31, one launch (start us, length us, event | category | flops | bytes accessed | tf_op | source)
XLA Modules:
  0.0 276.2 jit_solution(11449581989942818718)
XLA Ops:
  0.0 0.0 copy-start
  0.0 2.2 copy-done
  2.2 0.0 copy-start.1
  2.2 0.9 copy-done.1
  3.1 0.0 copy-start.2
  3.1 0.7 copy-done.2
  3.8 0.0 copy-start.3
  3.8 0.7 copy-done.3
  4.5 0.0 copy-start.4
  4.5 0.7 copy-done.4
  5.2 0.0 copy-start.5
  5.2 0.7 copy-done.5
  5.9 67.8 %exchange.1 = (bf16[8,2,32,32,128]{4,3,2,1,0:T(8,128)(2,1)S(1)}, bf16[8,2,8,32,128]{4,3,2,1,0:T(8,128)(2,1)S(1)}, s32[32,128]{1,0:T(8,128)S(1)}, f32[32,128]{1,0:T(8,128)S(1)}) custom-call(s32[4,16]{1,0:T(4,128)S(1)} %bitcast.19, f32[4,16]{1,0:T(4,128)S(1)} %bitcast.20, bf16[16,32,128]{2,1,0:T(8,128)(2,1)S(1)} %bitcast.16, ...), custom_call_target="tpu_custom_call" | custom-call | tf_op jit(solution)/shard_map/exchange/pallas_call | solution.py:262
  73.6 202.6 %products.1 = bf16[8,32,16384]{2,1,0:T(8,128)(2,1)} custom-call(s32[32,128]{1,0:T(8,128)S(1)} %get-tuple-element.9.cols, f32[32,128]{1,0:T(8,128)S(1)} %get-tuple-element.10.scale, bf16[8,2,8,32,128]{4,3,2,1,0:T(8,128)(2,1)S(1)} %get-tuple-element.11.a_ref, bf16[8,2,32,32,128]{4,3,2,1,0:T(8,128)(2,1)S(1)} %get-tuple-element.12.b_ref), custom_call_target="tpu_custom_call" | custom-call | tf_op jit(solution)/shard_map/products/pallas_call | solution.py:290
Async XLA Ops:
  0.0 2.2 copy-start
  2.2 0.9 copy-start.1
  3.1 0.7 copy-start.2
  3.8 0.7 copy-start.3
  4.5 0.7 copy-start.4
  5.2 0.7 copy-start.5

commit v2 on v1

v2 whole, which is shorter than its diff:
```python
import jax
import jax.numpy as jnp
from jax import lax
from jax.experimental import pallas as pl
from jax.experimental.pallas import tpu as pltpu
from jax.sharding import PartitionSpec as P

MESH = pl.DeviceIdType.MESH
F32, BF16, I32 = jnp.float32, jnp.bfloat16, jnp.int32

OFFSETS = ((1, 0), (0, 1), (3, 0), (1, 1), (2, 0), (3, 1), (2, 1), (0, 0))
HOPS = (1, 3, 2)


def lane_groups(v, group):
    low, high = group % 2 == 0, group < 2
    t = [None] * 4
    for i in (0, 2):
        t[i] = jnp.where(low, v[i], pltpu.roll(v[i + 1], 32, 1))
        t[i + 1] = jnp.where(low, pltpu.roll(v[i], 96, 1), v[i + 1])
    w = [None] * 4
    for i in (0, 1):
        w[i] = jnp.where(high, t[i], pltpu.roll(t[i + 2], 64, 1))
        w[i + 2] = jnp.where(high, pltpu.roll(t[i], 64, 1), t[i + 2])
    return w


def exchange_kernel(
    cols_ref, scale_ref, a_ref, b_ref, bs_ref, bc_ref,
    xout, ocols,
    b_vm, a_vm, bs_vm, bc_vm, cols_vm, scale_vm, bsend, brecv, arecv, xs,
    idx_s, idx_r, as_s, as_r, idx_sm, as_sm, ctable, stable, msend, mrecv, m_sm,
    local_sem, out_sem, msm_sem, idx_ss, idx_rs, as_ss, as_rs, b_ss, b_rs, m_ss, m_rs, a_ss, a_rs,
):
    c, r = lax.axis_index("col"), lax.axis_index("row")
    s, q = c // 2, c % 2
    z, xl, y, xh = s // 2, s % 2, r // 2, r % 2
    k = (s + r) % 8
    rx = y * 2 + (1 - xh)
    kx = (s + rx) % 8

    def dev(s_, q_, r_):
        return {"row": r_, "col": 2 * s_ + q_}

    def chip(d):
        dz, dx = OFFSETS[d]
        return ((z + dz) % 4) * 2 + (1 - xl if dx else xl)

    def chip_behind(d):
        dz, dx = OFFSETS[d]
        return ((z + 4 - dz) % 4) * 2 + (1 - xl if dx else xl)

    def row_at(dy):
        return ((y + dy) % 4) * 2 + xh

    def send(src, dst, ssem, rsem, target):
        return pltpu.make_async_remote_copy(
            src_ref=src, dst_ref=dst, send_sem=ssem, recv_sem=rsem, device_id=target, device_id_type=MESH
        )

    loads = [
        pltpu.make_async_copy(src, dst, local_sem.at[n])
        for n, (src, dst) in enumerate(
            ((cols_ref, cols_vm), (scale_ref, scale_vm), (a_ref, a_vm), (bs_ref, bs_vm), (bc_ref, bc_vm), (b_ref, b_vm))
        )
    ]
    for copy in loads:
        copy.start()

    barrier = pltpu.get_barrier_semaphore()
    peers = []
    for e in range(1, 8):
        peers.append(dev((s + 8 - e) % 8, q, (r + e) % 8))
    for d in range(7):
        for p in range(2):
            peers.append(dev(chip(d), p, r))
    peers.append(dev(s, 1 - q, r))
    for p in range(2):
        peers.append(dev(s, p, rx))
    for dy in HOPS:
        peers.append(dev(s, q, row_at(dy)))
    for peer in peers:
        pl.semaphore_signal(barrier, inc=1, device_id=peer, device_id_type=MESH)
    idx_s[...] = jnp.zeros_like(idx_s)
    as_s[...] = jnp.zeros_like(as_s)
    loads[0].wait()
    loads[1].wait()
    idx_s[0:4, 0:16] = cols_vm[...]
    as_s[0:4, 0:16] = scale_vm[...]
    loads[2].wait()
    pl.semaphore_wait(barrier, len(peers))

    idx_sends = []
    for e in range(1, 8):
        to = dev((s + 8 - e) % 8, q, (r + e) % 8)
        idx_sends.append(send(idx_s, idx_r.at[s], idx_ss.at[e - 1], idx_rs.at[s], to))
        idx_sends.append(send(as_s, as_r.at[s], as_ss.at[e - 1], as_rs.at[s], to))
    for copy in idx_sends:
        copy.start()

    own_rows = pl.ds(pl.multiple_of(q * 8, 8), 8)
    other_half = a_vm.at[pl.ds(pl.multiple_of((1 - q) * 8, 8), 8)]
    a_sends = [send(a_vm.at[pl.ds(p * 8, 8)], arecv.at[k, q], a_ss.at[1 + p], a_rs.at[1 + q], dev(s, p, rx)) for p in range(2)]
    a_sends.append(send(other_half, arecv.at[k, q], a_ss.at[0], a_rs.at[0], dev(s, 1 - q, r)))
    for copy in a_sends:
        copy.start()
    arecv[k, q] = a_vm[own_rows]

    idx_r[s] = idx_s[...]
    as_r[s] = as_s[...]
    loads[3].wait()
    loads[4].wait()
    for g in range(4):
        lanes = pl.ds(g * 128, 128)
        for src, table in ((bs_vm, stable), (bc_vm, ctable)):
            v = src[:, lanes].astype(F32)
            eights = [jnp.broadcast_to(v[n:n + 1, :], (8, 128)) for n in range(4)]
            table[lanes, :] = jnp.transpose(jnp.concatenate(eights * 4, axis=0))

    for e in range(1, 8):
        sb, rb = (s + e) % 8, (r + 8 - e) % 8
        send(idx_s, idx_r.at[sb], idx_ss.at[e - 1], idx_rs.at[sb], dev(sb, q, rb)).wait_recv()
        send(as_s, as_r.at[sb], as_ss.at[e - 1], as_rs.at[sb], dev(sb, q, rb)).wait_recv()
    to_smem = [pltpu.make_async_copy(idx_r, idx_sm, local_sem.at[6]), pltpu.make_async_copy(as_r, as_sm, local_sem.at[7])]
    for copy in to_smem:
        copy.start()
    for copy in to_smem:
        copy.wait()
    loads[5].wait()

    lane = lax.broadcasted_iota(I32, (1, 128), 1)
    slot_m, slot_i = lane // 32, lane % 8

    def metas(sd, p, out):
        def row_of(i, rows):
            srow, crow = rows
            for m in range(4):
                t = idx_sm[sd, m, p * 8 + i]
                here = (slot_m == m) & (slot_i == i)
                srow = jnp.where(here, stable[pl.ds(t, 1), :] * as_sm[sd, m, p * 8 + i], srow)
                crow = jnp.where(here, ctable[pl.ds(t, 1), :], crow)
            return srow, crow

        empty = jnp.zeros((1, 128), F32)
        srow, crow = lax.fori_loop(0, 8, row_of, (empty, empty))
        out[0:1, :] = srow
        out[1:2, :] = crow * 8.0

    def gather(sd, p, out):
        def rows_of(i, _):
            for m in range(4):
                out[i * 4 + m] = b_vm[idx_sm[sd, m, p * 8 + i]]
            return _

        lax.fori_loop(0, 8, rows_of, 0)

    b_sends, m_sends = [], []
    pending = []
    for d in range(7):
        sd = chip(d)
        for p in range(2):
            n = 2 * d + p
            gather(sd, p, bsend.at[n])
            metas(sd, p, msend.at[n])
            for copy in pending:
                copy.start()
            m_copy = send(msend.at[n], mrecv.at[k, q], m_ss.at[n], m_rs.at[k, q], dev(sd, p, r))
            b_copy = send(bsend.at[n], brecv.at[k, q], b_ss.at[n], b_rs.at[k, q], dev(sd, p, r))
            m_sends.append(m_copy)
            b_sends.append(b_copy)
            pending = [m_copy, b_copy]
    gather(s, 1 - q, bsend.at[14])
    metas(s, 1 - q, msend.at[14])
    for copy in pending:
        copy.start()
    gather(s, q, brecv.at[k, q])
    metas(s, q, mrecv.at[k, q])
    m_copy = send(msend.at[14], mrecv.at[k, q], m_ss.at[14], m_rs.at[k, q], dev(s, 1 - q, r))
    b_copy = send(bsend.at[14], brecv.at[k, q], b_ss.at[14], b_rs.at[k, q], dev(s, 1 - q, r))
    m_sends.append(m_copy)
    b_sends.append(b_copy)
    m_copy.start()
    b_copy.start()

    send(other_half, arecv.at[k, 1 - q], a_ss.at[0], a_rs.at[0], dev(s, 1 - q, r)).wait_recv()
    for p in range(2):
        send(other_half, arecv.at[kx, p], a_ss.at[1 + p], a_rs.at[1 + p], dev(s, p, rx)).wait_recv()
    for h, dy in enumerate(HOPS):
        for j, slot in enumerate((k, kx)):
            n = 3 + 2 * h + j
            copy = send(arecv.at[slot], arecv.at[slot], a_ss.at[n], a_rs.at[n], dev(s, q, row_at(dy)))
            copy.start()
            a_sends.append(copy)

    group = lax.broadcasted_iota(I32, (8, 128), 1) // 32
    quarter = lax.broadcasted_iota(I32, (32, 128), 1) // 32
    outs = []

    def process(kb, p):
        e = len(outs)
        scales = pltpu.make_async_copy(mrecv.at[kb, p], m_sm.at[e], msm_sem.at[e])
        scales.start()
        ocols[e:e + 1, :] = mrecv[kb, p, 1:2, :].astype(I32)
        return e, scales

    def products(e, scales, kb, p):
        scales.wait()
        if e >= 2:
            outs[e - 2].wait()
        x = xs.at[e % 2]

        def row(i, _):
            a = arecv[kb, p, i]
            zero = jnp.zeros_like(a)
            left = jnp.concatenate([jnp.where(quarter == m, a, zero) for m in range(4)], axis=0)
            right = brecv[kb, p, pl.ds(i * 4, 4)].reshape(128, 128)
            prod = jnp.dot(left, right, preferred_element_type=F32)
            for m in range(4):
                rows = [prod[m * 32 + h * 8:m * 32 + h * 8 + 8, :] for h in range(4)]
                for n, block in enumerate(lane_groups(rows, group)):
                    w = m * 4 + n
                    x[i, w] = block * m_sm[e, 0, w * 8 + i]
            return _

        lax.fori_loop(0, 8, row, 0)
        copy = pltpu.make_async_copy(x, xout.at[e], out_sem.at[e])
        copy.start()
        outs.append(copy)

    e, scales = process(k, q)
    products(e, scales, k, q)
    n_other = 1 - q
    send(msend.at[14], mrecv.at[k, n_other], m_ss.at[14], m_rs.at[k, n_other], dev(s, n_other, r)).wait_recv()
    e, scales = process(k, n_other)
    send(bsend.at[14], brecv.at[k, n_other], b_ss.at[14], b_rs.at[k, n_other], dev(s, n_other, r)).wait_recv()
    products(e, scales, k, n_other)
    for h, dy in enumerate(HOPS):
        rb = row_at(4 - dy)
        for j, rr in enumerate((rb, (rb // 2) * 2 + (1 - xh))):
            slot = (s + rr) % 8
            n = 3 + 2 * h + j
            send(arecv.at[slot], arecv.at[slot], a_ss.at[n], a_rs.at[n], dev(s, q, rb)).wait_recv()
    for d in range(7):
        sb = chip_behind(d)
        kb = (sb + r) % 8
        for p in range(2):
            n = 2 * d + p
            send(msend.at[n], mrecv.at[kb, p], m_ss.at[n], m_rs.at[kb, p], dev(sb, p, r)).wait_recv()
            e, scales = process(kb, p)
            send(bsend.at[n], brecv.at[kb, p], b_ss.at[n], b_rs.at[kb, p], dev(sb, p, r)).wait_recv()
            products(e, scales, kb, p)
    for copy in idx_sends + a_sends + b_sends + m_sends:
        copy.wait_send()
    for copy in outs[14:]:
        copy.wait()


def scatter_kernel(cols, x_ref, out_ref, *accs):
    g = pl.program_id(0)
    group = lax.broadcasted_iota(I32, (8, 128), 1) // 32

    @pl.when(g == 0)
    def _():
        def clear(t, _):
            for acc in accs:
                acc[pl.ds(t * 64, 64), :] = jnp.zeros((64, 128), F32)
            return _

        lax.fori_loop(0, 64, clear, 0)

    @pl.when(g < 16)
    def _():
        def scatter(w4, _):
            for ww in range(4):
                w = w4 * 4 + ww
                at = [pl.ds(pl.multiple_of(cols[g, w * 8 + i], 8), 8) for i in range(8)]
                new = [acc[at[i], :] + x_ref[0, i, w] for i, acc in enumerate(accs)]
                for i, acc in enumerate(accs):
                    acc[at[i], :] = new[i]
            return _

        lax.fori_loop(0, 4, scatter, 0)

    for i, acc in enumerate(accs):
        @pl.when(g == 16 + i)
        def _(acc=acc):
            def tile(t, _):
                tiles = []
                for u in range(8):
                    base = pl.multiple_of((t * 8 + u) * 32, 32)
                    tiles.append(lane_groups([acc[pl.ds(base + n * 8, 8), :] for n in range(4)], group))
                for h in range(4):
                    row = jnp.concatenate([w[h] for w in tiles], axis=1).astype(BF16)
                    out_ref[0, h * 8:h * 8 + 8, pl.ds(pl.multiple_of(t * 1024, 1024), 1024)] = row
                return _

            lax.fori_loop(0, 16, tile, 0)


def on_device(a_blocks, a_scale, a_cols, b_blocks, b_scale, b_cols):
    hbm = pl.BlockSpec(memory_space=pltpu.HBM)
    dma = pltpu.SemaphoreType.DMA
    x, cols = pl.pallas_call(
        exchange_kernel,
        name="exchange",
        out_shape=(
            jax.ShapeDtypeStruct((16, 8, 16, 8, 128), F32),
            jax.ShapeDtypeStruct((16, 128), I32),
        ),
        in_specs=[hbm] * 6,
        out_specs=(hbm, pl.BlockSpec(memory_space=pltpu.VMEM)),
        scratch_shapes=[
            pltpu.VMEM((512, 32, 128), BF16),
            pltpu.VMEM((16, 32, 128), BF16),
            pltpu.VMEM((4, 512), F32),
            pltpu.VMEM((4, 512), I32),
            pltpu.VMEM((4, 16), I32),
            pltpu.VMEM((4, 16), F32),
            pltpu.VMEM((15, 32, 32, 128), BF16),
            pltpu.VMEM((8, 2, 32, 32, 128), BF16),
            pltpu.VMEM((8, 2, 8, 32, 128), BF16),
            pltpu.VMEM((2, 8, 16, 8, 128), F32),
            pltpu.VMEM((8, 128), I32),
            pltpu.VMEM((8, 8, 128), I32),
            pltpu.VMEM((8, 128), F32),
            pltpu.VMEM((8, 8, 128), F32),
            pltpu.SMEM((8, 8, 128), I32),
            pltpu.SMEM((8, 8, 128), F32),
            pltpu.VMEM((512, 128), F32),
            pltpu.VMEM((512, 128), F32),
            pltpu.VMEM((15, 8, 128), F32),
            pltpu.VMEM((8, 2, 8, 128), F32),
            pltpu.SMEM((16, 8, 128), F32),
            dma((8,)), dma((16,)), dma((16,)), dma((7,)), dma((8,)), dma((7,)), dma((8,)),
            dma((15,)), dma((8, 2)), dma((15,)), dma((8, 2)), dma((9,)), dma((9,)),
        ],
        compiler_params=pltpu.CompilerParams(collective_id=0, has_side_effects=True, vmem_limit_bytes=67043328),
    )(a_cols[0, 0].T, a_scale[0, 0].T, a_blocks[0, 0], b_blocks[0, 0], b_scale[0, 0].T, b_cols[0, 0].T)
    out = pl.pallas_call(
        scatter_kernel,
        name="scatter",
        grid=(24,),
        out_shape=jax.ShapeDtypeStruct((8, 32, 16384), BF16),
        in_specs=[
            pl.BlockSpec(memory_space=pltpu.SMEM),
            pl.BlockSpec((1, 8, 16, 8, 128), lambda g: (jnp.minimum(g, 15), 0, 0, 0, 0)),
        ],
        out_specs=pl.BlockSpec((1, 32, 16384), lambda g: (jnp.maximum(g - 16, 0), 0, 0)),
        scratch_shapes=[pltpu.VMEM((4096, 128), F32)] * 8,
        compiler_params=pltpu.CompilerParams(vmem_limit_bytes=32 << 20),
    )(cols, x)
    return out[None, None]


def solution(mesh):
    blocks = P("col", "row", None, None, None)
    small = P("col", "row", None, None)
    return jax.shard_map(
        on_device,
        mesh=mesh,
        in_specs=(blocks, small, small, blocks, small, small),
        out_specs=blocks,
        check_vma=False,
    )
```

time: 278 us -> 138 us (0.50)
  the two profiles are of different devices: /device:TPU:31 before, /device:TPU:65 now
where the time goes in v2:
time: 138 us
  Pallas kernels  134 us (97%)
  local copies, waits for them, and re-layouts  4.07 us (3%)
    pallas_call x1, Pallas kernels, on_device(): pl.pallas_call(exchange_kernel, name='exchange', out_shape=(jax.ShapeDtyp...  104 us
    pallas_call x1, Pallas kernels, on_device(): pl.pallas_call(scatter_kernel, name='scatter', grid=(24,), out_shape=jax....  29.9 us
    unnamed x4, local copies, waits for them, and re-layouts  4.07 us

profile of v2, /device:TPU:65, one launch (start us, length us, event | category | flops | bytes accessed | tf_op | source)
XLA Modules:
  0.0 137.8 jit_solution(6120642899528853998)
XLA Ops:
  0.0 103.8 %exchange.1 = (f32[16,8,16,8,128]{4,3,2,1,0:T(8,128)}, s32[16,128]{1,0:T(8,128)}) custom-call(s32[4,16]{1,0:T(4,128)} %bitcast.19, f32[4,16]{1,0:T(4,128)} %bitcast.20, bf16[16,32,128]{2,1,0:T(8,128)(2,1)} %bitcast.16, bf16[512,32,128]{2,1,0:T(8,128)(2,1)} %bitcast.15, f32[4,512]{1,0:T(4,128)} %bitcast.17, s32[4,512]{1,0:T(4,128)} %bitcast.18), custom_call_target="tpu_custom_call" | custom-call | tf_op jit(solution)/shard_map/exchange/pallas_call | solution.py:303
  103.8 0.0 copy-start
  103.9 3.4 %copy-done = f32[16,8,16,8,128]{4,3,2,1,0:T(8,128)S(1)} copy-done((f32[16,8,16,8,128]{4,3,2,1,0:T(8,128)S(1)}, f32[16,8,16,8,128]{4,3,2,1,0:T(8,128)}, u32[]{:S(2)}) %copy-start) | copy-done | bytes 8388632
  107.2 0.0 copy-start.1
  107.2 0.7 copy-done.1
  107.9 29.9 %scatter.1 = bf16[8,32,16384]{2,1,0:T(8,128)(2,1)} custom-call(s32[16,128]{1,0:T(8,128)S(1)} %copy-done.1, f32[16,8,16,8,128]{4,3,2,1,0:T(8,128)S(1)} %copy-done), custom_call_target="tpu_custom_call" | custom-call | tf_op jit(solution)/shard_map/scatter/pallas_call | solution.py:339
Async XLA Ops:
  103.8 3.4 %copy-start = (f32[16,8,16,8,128]{4,3,2,1,0:T(8,128)S(1)}, f32[16,8,16,8,128]{4,3,2,1,0:T(8,128)}, u32[]{:S(2)}) copy-start(f32[16,8,16,8,128]{4,3,2,1,0:T(8,128)} %get-tuple-element.8.x_ref) | copy-start | bytes 25165828
  107.2 0.7 copy-start.1

commit v3 on v2

v3 whole, which is shorter than its diff:
```python
import jax
import jax.numpy as jnp
from jax import lax
from jax.experimental import pallas as pl
from jax.experimental.pallas import tpu as pltpu
from jax.sharding import PartitionSpec as P

MESH = pl.DeviceIdType.MESH
F32, BF16, I32 = jnp.float32, jnp.bfloat16, jnp.int32

HOPS = (1, 3, 2)
CHIPS = (0, 7, 3, 5, 6, 2, 4, 1)


def lane_groups(v, low, high):
    t = [None] * 4
    for i in (0, 2):
        t[i] = jnp.where(low, v[i], pltpu.roll(v[i + 1], 32, 1))
        t[i + 1] = jnp.where(low, pltpu.roll(v[i], 96, 1), v[i + 1])
    w = [None] * 4
    for i in (0, 1):
        w[i] = jnp.where(high, t[i], pltpu.roll(t[i + 2], 64, 1))
        w[i + 2] = jnp.where(high, pltpu.roll(t[i], 64, 1), t[i + 2])
    return w


def exchange_kernel(
    cols_ref, scale_ref, a_ref, b_ref, bs_ref, bc_ref,
    xout, ocols,
    b_vm, a_vm, bs_vm, bc_vm, cols_vm, scale_vm, bsend, brecv, arecv, prods, xs,
    idx_s, idx_r, as_s, as_r, idx_sm, as_sm, ctable, stable, msend, mrecv, m_sm,
    local_sem, out_sem, msm_sem, idx_ss, idx_rs, as_ss, as_rs, b_ss, b_rs, m_ss, m_rs, a_ss, a_rs,
):
    c, r = lax.axis_index("col"), lax.axis_index("row")
    s, q = c // 2, c % 2
    z, xl, y, xh = s // 2, s % 2, r // 2, r % 2
    k = (s + r) % 8
    rx = y * 2 + (1 - xh)
    kx = (s + rx) % 8

    def dev(s_, q_, r_):
        return {"row": r_, "col": 2 * s_ + q_}

    def hop(e):
        t = (e // 2) % 8
        f = t * 0
        for n, number in enumerate(CHIPS):
            f = jnp.where(t == n, number, f)
        dx, h = f % 2, f // 2
        return h + h // 2 - 2 * (h // 3), xl + dx - 2 * xl * dx

    def chip(e):
        dz, x = hop(e)
        return ((z + dz) % 4) * 2 + x

    def chip_behind(e):
        dz, x = hop(e)
        return ((z + 4 - dz) % 4) * 2 + x

    def core(e):
        return (q + e) % 2

    def row_at(dy):
        return ((y + dy) % 4) * 2 + xh

    def send(src, dst, ssem, rsem, target):
        return pltpu.make_async_remote_copy(
            src_ref=src, dst_ref=dst, send_sem=ssem, recv_sem=rsem, device_id=target, device_id_type=MESH
        )

    loads = [
        pltpu.make_async_copy(src, dst, local_sem.at[n])
        for n, (src, dst) in enumerate(
            ((cols_ref, cols_vm), (scale_ref, scale_vm), (a_ref, a_vm), (bs_ref, bs_vm), (bc_ref, bc_vm), (b_ref, b_vm))
        )
    ]
    for copy in loads:
        copy.start()

    barrier = pltpu.get_barrier_semaphore()
    peers = []
    for e in range(1, 8):
        peers.append(dev((s + 8 - e) % 8, q, (r + e) % 8))
    for e in range(1, 16):
        peers.append(dev(chip(e), core(e), r))
    for p in range(2):
        peers.append(dev(s, p, rx))
    for dy in HOPS:
        peers.append(dev(s, q, row_at(dy)))
    for peer in peers:
        pl.semaphore_signal(barrier, inc=1, device_id=peer, device_id_type=MESH)
    idx_s[...] = jnp.zeros_like(idx_s)
    as_s[...] = jnp.zeros_like(as_s)
    loads[0].wait()
    loads[1].wait()
    for p in range(2):
        idx_s[p * 4:p * 4 + 4, 0:8] = cols_vm[:, p * 8:p * 8 + 8]
        as_s[p * 4:p * 4 + 4, 0:8] = scale_vm[:, p * 8:p * 8 + 8]
    loads[2].wait()
    pl.semaphore_wait(barrier, len(peers))

    idx_sends = []
    for e in range(1, 8):
        to = dev((s + 8 - e) % 8, q, (r + e) % 8)
        idx_sends.append(send(idx_s, idx_r.at[s], idx_ss.at[e - 1], idx_rs.at[s], to))
        idx_sends.append(send(as_s, as_r.at[s], as_ss.at[e - 1], as_rs.at[s], to))
    for copy in idx_sends:
        copy.start()

    own_rows = pl.ds(pl.multiple_of(q * 8, 8), 8)
    other_half = a_vm.at[pl.ds(pl.multiple_of((1 - q) * 8, 8), 8)]
    a_sends = [send(a_vm.at[pl.ds(p * 8, 8)], arecv.at[k, q], a_ss.at[1 + p], a_rs.at[1 + q], dev(s, p, rx)) for p in range(2)]
    a_sends.append(send(other_half, arecv.at[k, q], a_ss.at[0], a_rs.at[0], dev(s, 1 - q, r)))
    for copy in a_sends:
        copy.start()
    arecv[k, q] = a_vm[own_rows]

    idx_r[s] = idx_s[...]
    as_r[s] = as_s[...]
    loads[3].wait()
    loads[4].wait()
    for g in range(4):
        lanes = pl.ds(g * 128, 128)
        for src, table in ((bs_vm, stable), (bc_vm, ctable)):
            v = src[:, lanes].astype(F32)
            eights = [jnp.broadcast_to(v[n:n + 1, :], (8, 128)) for n in range(4)]
            table[lanes, :] = jnp.transpose(jnp.concatenate(eights * 4, axis=0))

    for e in range(1, 8):
        sb, rb = (s + e) % 8, (r + 8 - e) % 8
        send(idx_s, idx_r.at[sb], idx_ss.at[e - 1], idx_rs.at[sb], dev(sb, q, rb)).wait_recv()
        send(as_s, as_r.at[sb], as_ss.at[e - 1], as_rs.at[sb], dev(sb, q, rb)).wait_recv()
    to_smem = [pltpu.make_async_copy(idx_r, idx_sm, local_sem.at[6]), pltpu.make_async_copy(as_r, as_sm, local_sem.at[7])]
    for copy in to_smem:
        copy.start()
    for copy in to_smem:
        copy.wait()
    loads[5].wait()

    lane = lax.broadcasted_iota(I32, (1, 128), 1)
    place = lane // 32 * 8 + lane % 8

    def to_peer(e):
        target = dev(chip(e), core(e), r)
        n = e - 2
        return (
            send(msend.at[n], mrecv.at[k, q], m_ss.at[n], m_rs.at[k, q], target),
            send(bsend.at[n], brecv.at[k, q], b_ss.at[n], b_rs.at[k, q], target),
        )

    def pick(e, carry):
        sd, p, n = chip(e), core(e), e - 2
        srow = crow = jnp.zeros((1, 128), F32)
        for i in range(8):
            for m in range(4):
                t = idx_sm[sd, p * 4 + m, i]
                bsend[n, i * 4 + m] = b_vm[t]
                here = place == m * 8 + i
                srow = jnp.where(here, stable[pl.ds(t, 1), :] * as_sm[sd, p * 4 + m, i], srow)
                crow = jnp.where(here, ctable[pl.ds(t, 1), :], crow)
        msend[n, 0:1, :] = srow
        msend[n, 1:2, :] = crow * 8.0

        @pl.when((e > 2) & (e < 17))
        def _():
            for copy in to_peer(e - 1):
                copy.start()

        return carry

    lax.fori_loop(2, 18, pick, 0)
    for copy in to_peer(17):
        copy.start()
    own = [
        pltpu.make_async_copy(msend.at[14], mrecv.at[k, q], local_sem.at[8]),
        pltpu.make_async_copy(bsend.at[14], brecv.at[k, q], local_sem.at[9]),
    ]
    for copy in own:
        copy.start()

    send(other_half, arecv.at[k, 1 - q], a_ss.at[0], a_rs.at[0], dev(s, 1 - q, r)).wait_recv()
    for p in range(2):
        send(other_half, arecv.at[kx, p], a_ss.at[1 + p], a_rs.at[1 + p], dev(s, p, rx)).wait_recv()
    for h, dy in enumerate(HOPS):
        for j, slot in enumerate((k, kx)):
            n = 3 + 2 * h + j
            copy = send(arecv.at[slot], arecv.at[slot], a_ss.at[n], a_rs.at[n], dev(s, q, row_at(dy)))
            copy.start()
            a_sends.append(copy)
    for copy in own:
        copy.wait()

    group = lax.broadcasted_iota(I32, (8, 128), 1) // 32
    low, high = group % 2 == 0, group < 2
    quarter = lax.broadcasted_iota(I32, (32, 128), 1) // 32

    def out_copy(e):
        return pltpu.make_async_copy(xs.at[e % 2], xout.at[e], out_sem.at[e])

    def process(e, carry):
        sb, p = chip_behind(e), core(e)
        kb = (sb + r) % 8
        source = dev(sb, p, r)

        @pl.when(e > 0)
        def _():
            send(msend.at[0], mrecv.at[kb, p], m_ss.at[0], m_rs.at[kb, p], source).wait_recv()

        scales = pltpu.make_async_copy(mrecv.at[kb, p], m_sm.at[e], msm_sem.at[e])
        scales.start()
        ocols[pl.ds(e, 1), :] = mrecv[kb, p, 1:2, :].astype(I32)

        @pl.when(e == 2)
        def _():
            for h, dy in enumerate(HOPS):
                rb = row_at(4 - dy)
                for j, rr in enumerate((rb, (rb // 2) * 2 + (1 - xh))):
                    slot = (s + rr) % 8
                    n = 3 + 2 * h + j
                    send(arecv.at[slot], arecv.at[slot], a_ss.at[n], a_rs.at[n], dev(s, q, rb)).wait_recv()

        @pl.when(e > 0)
        def _():
            send(bsend.at[0], brecv.at[kb, p], b_ss.at[0], b_rs.at[kb, p], source).wait_recv()

        for i in range(8):
            a = arecv[kb, p, i]
            zero = jnp.zeros_like(a)
            left = jnp.concatenate([jnp.where(quarter == m, a, zero) for m in range(4)], axis=0)
            right = brecv[kb, p, i * 4:i * 4 + 4].reshape(128, 128)
            prods[i] = jnp.dot(left, right, preferred_element_type=F32)
        scales.wait()

        @pl.when(e >= 2)
        def _():
            out_copy(e - 2).wait()

        for i in range(8):
            for m in range(4):
                rows = [prods[i, m * 32 + h * 8:m * 32 + h * 8 + 8, :] for h in range(4)]
                for n, block in enumerate(lane_groups(rows, low, high)):
                    w = m * 4 + n
                    xs[e % 2, i, w] = block * m_sm[e, 0, w * 8 + i]
        out_copy(e).start()
        return carry

    lax.fori_loop(0, 16, process, 0)
    for copy in idx_sends + a_sends:
        copy.wait_send()
    for e in range(2, 18):
        if e != 16:
            for copy in to_peer(e):
                copy.wait_send()
    for e in (14, 15):
        out_copy(e).wait()


def scatter_kernel(cols, x_ref, out_ref, x, sem, *accs):
    g = pl.program_id(0)

    @pl.when(g == 0)
    def _():
        def load(e):
            return pltpu.make_async_copy(x_ref.at[e], x.at[e], sem.at[e])

        for e in range(16):
            load(e).start()

        def clear(t, _):
            for acc in accs:
                acc[pl.ds(pl.multiple_of(t * 64, 64), 64), :] = jnp.zeros((64, 128), F32)
            return _

        lax.fori_loop(0, 64, clear, 0)

        def add(e, _):
            load(e).wait()
            for w in range(16):
                at = [pl.ds(pl.multiple_of(cols[e, w * 8 + i], 8), 8) for i in range(8)]
                new = [acc[at[i], :] + x[e, i, w] for i, acc in enumerate(accs)]
                for i, acc in enumerate(accs):
                    acc[at[i], :] = new[i]
            return _

        lax.fori_loop(0, 16, add, 0)

    group = lax.broadcasted_iota(I32, (16, 128), 1) // 32
    low, high = group % 2 == 0, group < 2
    for i, acc in enumerate(accs):
        @pl.when(g == i)
        def _(acc=acc):
            def tile(t, _):
                for u in range(8):
                    base = pl.multiple_of((t * 8 + u) * 64, 64)
                    v = [
                        jnp.concatenate([acc[pl.ds(base + n * 8, 8), :], acc[pl.ds(base + 32 + n * 8, 8), :]], axis=0).astype(BF16)
                        for n in range(4)
                    ]
                    w = lane_groups(v, low, high)
                    for h in range(4):
                        lanes = pl.ds(pl.multiple_of((t * 8 + u) * 256, 256), 256)
                        out_ref[0, h * 8:h * 8 + 8, lanes] = jnp.concatenate([w[h][0:8], w[h][8:16]], axis=1)
                return _

            lax.fori_loop(0, 8, tile, 0)


def on_device(a_blocks, a_scale, a_cols, b_blocks, b_scale, b_cols):
    hbm = pl.BlockSpec(memory_space=pltpu.HBM)
    dma = pltpu.SemaphoreType.DMA
    x, cols = pl.pallas_call(
        exchange_kernel,
        name="exchange",
        out_shape=(
            jax.ShapeDtypeStruct((16, 8, 16, 8, 128), F32),
            jax.ShapeDtypeStruct((16, 128), I32),
        ),
        in_specs=[hbm] * 6,
        out_specs=(hbm, pl.BlockSpec(memory_space=pltpu.VMEM)),
        scratch_shapes=[
            pltpu.VMEM((512, 32, 128), BF16),
            pltpu.VMEM((16, 32, 128), BF16),
            pltpu.VMEM((4, 512), F32),
            pltpu.VMEM((4, 512), I32),
            pltpu.VMEM((4, 16), I32),
            pltpu.VMEM((4, 16), F32),
            pltpu.VMEM((16, 32, 32, 128), BF16),
            pltpu.VMEM((8, 2, 32, 32, 128), BF16),
            pltpu.VMEM((8, 2, 8, 32, 128), BF16),
            pltpu.VMEM((8, 128, 128), F32),
            pltpu.VMEM((2, 8, 16, 8, 128), F32),
            pltpu.VMEM((8, 128), I32),
            pltpu.VMEM((8, 8, 128), I32),
            pltpu.VMEM((8, 128), F32),
            pltpu.VMEM((8, 8, 128), F32),
            pltpu.SMEM((8, 8, 128), I32),
            pltpu.SMEM((8, 8, 128), F32),
            pltpu.VMEM((512, 128), F32),
            pltpu.VMEM((512, 128), F32),
            pltpu.VMEM((16, 8, 128), F32),
            pltpu.VMEM((8, 2, 8, 128), F32),
            pltpu.SMEM((16, 8, 128), F32),
            dma((10,)), dma((16,)), dma((16,)), dma((7,)), dma((8,)), dma((7,)), dma((8,)),
            dma((16,)), dma((8, 2)), dma((16,)), dma((8, 2)), dma((9,)), dma((9,)),
        ],
        compiler_params=pltpu.CompilerParams(collective_id=0, has_side_effects=True, vmem_limit_bytes=67043328),
    )(a_cols[0, 0].T, a_scale[0, 0].T, a_blocks[0, 0], b_blocks[0, 0], b_scale[0, 0].T, b_cols[0, 0].T)
    out = pl.pallas_call(
        scatter_kernel,
        name="scatter",
        grid=(8,),
        out_shape=jax.ShapeDtypeStruct((8, 32, 16384), BF16),
        in_specs=[pl.BlockSpec(memory_space=pltpu.SMEM), hbm],
        out_specs=pl.BlockSpec((1, 32, 16384), lambda g: (g, 0, 0)),
        scratch_shapes=[pltpu.VMEM((16, 8, 16, 8, 128), F32), dma((16,))] + [pltpu.VMEM((4096, 128), F32)] * 8,
        compiler_params=pltpu.CompilerParams(vmem_limit_bytes=67043328),
    )(cols, x)
    return out[None, None]


def solution(mesh):
    blocks = P("col", "row", None, None, None)
    small = P("col", "row", None, None)
    return jax.shard_map(
        on_device,
        mesh=mesh,
        in_specs=(blocks, small, small, blocks, small, small),
        out_specs=blocks,
        check_vma=False,
    )
```

time: 138 us -> 94.2 us (0.68)
  the two profiles are of different devices: /device:TPU:65 before, /device:TPU:31 now
where the time goes in v3:
time: 94.2 us; the launch traced here: 94 us
  Pallas kernels  94 us (100%)
    pallas_call x1, Pallas kernels, on_device(): pl.pallas_call(exchange_kernel, name='exchange', out_shape=(jax.ShapeDtyp...  77 us
    pallas_call x1, Pallas kernels, on_device(): pl.pallas_call(scatter_kernel, name='scatter', grid=(8,), out_shape=jax.S...  17 us

profile of v3, /device:TPU:31, one launch (start us, length us, event | category | flops | bytes accessed | tf_op | source)
XLA Modules:
  0.0 94.0 jit_solution(14377138641117335469)
XLA Ops:
  0.0 77.0 %exchange.1 = (f32[16,8,16,8,128]{4,3,2,1,0:T(8,128)}, s32[16,128]{1,0:T(8,128)}) custom-call(s32[4,16]{1,0:T(4,128)} %bitcast.19, f32[4,16]{1,0:T(4,128)} %bitcast.20, bf16[16,32,128]{2,1,0:T(8,128)(2,1)} %bitcast.16, bf16[512,32,128]{2,1,0:T(8,128)(2,1)} %bitcast.15, f32[4,512]{1,0:T(4,128)} %bitcast.17, s32[4,512]{1,0:T(4,128)} %bitcast.18), custom_call_target="tpu_custom_call" | custom-call | tf_op jit(solution)/shard_map/exchange/pallas_call | solution.py:311
  77.0 17.0 %scatter.1 = bf16[8,32,16384]{2,1,0:T(8,128)(2,1)} custom-call(s32[16,128]{1,0:T(8,128)} %get-tuple-element.7.cols, f32[16,8,16,8,128]{4,3,2,1,0:T(8,128)} %get-tuple-element.8.x_ref), custom_call_target="tpu_custom_call" | custom-call | tf_op jit(solution)/shard_map/scatter/pallas_call | solution.py:348

commit v4 on v3

--- a/solution.py
+++ b/solution.py
@@ -9,19 +9,18 @@
 F32, BF16, I32 = jnp.float32, jnp.bfloat16, jnp.int32
 
 HOPS = (1, 3, 2)
-CHIPS = (0, 7, 3, 5, 6, 2, 4, 1)
+CHIPS = (0, 7, 6, 3, 5, 2, 4, 1)
 
 
 def lane_groups(v, low, high):
-    t = [None] * 4
+    t, w = [None] * 4, [None] * 4
     for i in (0, 2):
-        t[i] = jnp.where(low, v[i], pltpu.roll(v[i + 1], 32, 1))
-        t[i + 1] = jnp.where(low, pltpu.roll(v[i], 96, 1), v[i + 1])
-    w = [None] * 4
+        turned = pltpu.roll(jnp.where(low, v[i + 1], v[i]), 32, 1)
+        t[i], t[i + 1] = jnp.where(low, v[i], turned), jnp.where(low, turned, v[i + 1])
     for i in (0, 1):
-        w[i] = jnp.where(high, t[i], pltpu.roll(t[i + 2], 64, 1))
-        w[i + 2] = jnp.where(high, pltpu.roll(t[i], 64, 1), t[i + 2])
-    return w
+        turned = pltpu.roll(jnp.where(high, t[i + 2], t[i]), 64, 1)
+        w[i], w[i + 2] = jnp.where(high, t[i], turned), jnp.where(high, turned, t[i + 2])
+    return [w[0], jnp.where(low, w[3], w[1]), w[2], jnp.where(low, w[1], w[3])]
 
 
 def exchange_kernel(
@@ -197,7 +196,19 @@
     def out_copy(e):
         return pltpu.make_async_copy(xs.at[e % 2], xout.at[e], out_sem.at[e])
 
-    def process(e, carry):
+    def scales_copy(e):
+        sb, p = chip_behind(e), core(e)
+        return pltpu.make_async_copy(mrecv.at[(sb + r) % 8, p], m_sm.at[e], msm_sem.at[e])
+
+    def finish(e):
+        for i in range(8):
+            for m in range(4):
+                rows = [prods[e % 2, i, m * 32 + h * 8:m * 32 + h * 8 + 8, :] for h in range(4)]
+                for n, block in enumerate(lane_groups(rows, low, high)):
+                    w = m * 4 + n
+                    xs[e % 2, i, w] = block * m_sm[e, 0, w * 8 + i]
+
+    def process(e, carry, late=True):
         sb, p = chip_behind(e), core(e)
         kb = (sb + r) % 8
         source = dev(sb, p, r)
@@ -206,8 +217,7 @@
         def _():
             send(msend.at[0], mrecv.at[kb, p], m_ss.at[0], m_rs.at[kb, p], source).wait_recv()
 
-        scales = pltpu.make_async_copy(mrecv.at[kb, p], m_sm.at[e], msm_sem.at[e])
-        scales.start()
+        scales_copy(e).start()
         ocols[pl.ds(e, 1), :] = mrecv[kb, p, 1:2, :].astype(I32)
 
         @pl.when(e == 2)
@@ -223,28 +233,31 @@
         def _():
             send(bsend.at[0], brecv.at[kb, p], b_ss.at[0], b_rs.at[kb, p], source).wait_recv()
 
+        if late:
+            scales_copy(e - 1).wait()
+
+            @pl.when(e >= 3)
+            def _():
+                out_copy(e - 3).wait()
+
+        if late:
+            finish(e - 1)
         for i in range(8):
             a = arecv[kb, p, i]
             zero = jnp.zeros_like(a)
             left = jnp.concatenate([jnp.where(quarter == m, a, zero) for m in range(4)], axis=0)
             right = brecv[kb, p, i * 4:i * 4 + 4].reshape(128, 128)
-            prods[i] = jnp.dot(left, right, preferred_element_type=F32)
-        scales.wait()
-
-        @pl.when(e >= 2)
-        def _():
-            out_copy(e - 2).wait()
-
-        for i in range(8):
-            for m in range(4):
-                rows = [prods[i, m * 32 + h * 8:m * 32 + h * 8 + 8, :] for h in range(4)]
-                for n, block in enumerate(lane_groups(rows, low, high)):
-                    w = m * 4 + n
-                    xs[e % 2, i, w] = block * m_sm[e, 0, w * 8 + i]
-        out_copy(e).start()
+            prods[e % 2, i] = jnp.dot(left, right, preferred_element_type=F32)
+        if late:
+            out_copy(e - 1).start()
         return carry
 
-    lax.fori_loop(0, 16, process, 0)
+    process(0, 0, late=False)
+    lax.fori_loop(1, 16, process, 0)
+    scales_copy(15).wait()
+    out_copy(13).wait()
+    finish(15)
+    out_copy(15).start()
     for copy in idx_sends + a_sends:
         copy.wait_send()
     for e in range(2, 18):
@@ -327,7 +340,7 @@
             pltpu.VMEM((16, 32, 32, 128), BF16),
             pltpu.VMEM((8, 2, 32, 32, 128), BF16),
             pltpu.VMEM((8, 2, 8, 32, 128), BF16),
-            pltpu.VMEM((8, 128, 128), F32),
+            pltpu.VMEM((2, 8, 128, 128), F32),
             pltpu.VMEM((2, 8, 16, 8, 128), F32),
             pltpu.VMEM((8, 128), I32),
             pltpu.VMEM((8, 8, 128), I32),

time: 94.2 us -> 86.8 us (0.921)
  Pallas kernels: 94 us -> 86.2 us
    pallas_call x1, Pallas kernels: 77 us -> 70.1 us  [on_device(): pl.pallas_call(exchange_kernel, name='exchange', out_shape=(jax.ShapeDtyp...]
where the time goes in v4:
time: 86.8 us; the launch traced here: 86.2 us
  Pallas kernels  86.2 us (99%)
    pallas_call x1, Pallas kernels, on_device(): pl.pallas_call(exchange_kernel, name='exchange', out_shape=(jax.ShapeDtyp...  70.1 us
    pallas_call x1, Pallas kernels, on_device(): pl.pallas_call(scatter_kernel, name='scatter', grid=(8,), out_shape=jax.S...  16.1 us

profile of v4, /device:TPU:31, one launch (start us, length us, event | category | flops | bytes accessed | tf_op | source)
XLA Modules:
  0.0 86.2 jit_solution(12787889097449225152)
XLA Ops:
  0.0 70.1 %exchange.1 = (f32[16,8,16,8,128]{4,3,2,1,0:T(8,128)}, s32[16,128]{1,0:T(8,128)}) custom-call(s32[4,16]{1,0:T(4,128)} %bitcast.19, f32[4,16]{1,0:T(4,128)} %bitcast.20, bf16[16,32,128]{2,1,0:T(8,128)(2,1)} %bitcast.16, bf16[512,32,128]{2,1,0:T(8,128)(2,1)} %bitcast.15, f32[4,512]{1,0:T(4,128)} %bitcast.17, s32[4,512]{1,0:T(4,128)} %bitcast.18), custom_call_target="tpu_custom_call" | custom-call | tf_op jit(solution)/shard_map/exchange/pallas_call | solution.py:324
  70.1 16.1 %scatter.1 = bf16[8,32,16384]{2,1,0:T(8,128)(2,1)} custom-call(s32[16,128]{1,0:T(8,128)} %get-tuple-element.7.cols, f32[16,8,16,8,128]{4,3,2,1,0:T(8,128)} %get-tuple-element.8.x_ref), custom_call_target="tpu_custom_call" | custom-call | tf_op jit(solution)/shard_map/scatter/pallas_call | solution.py:361

commit v5 on v4

--- a/solution.py
+++ b/solution.py
@@ -25,10 +25,10 @@
 
 def exchange_kernel(
     cols_ref, scale_ref, a_ref, b_ref, bs_ref, bc_ref,
-    xout, ocols,
-    b_vm, a_vm, bs_vm, bc_vm, cols_vm, scale_vm, bsend, brecv, arecv, prods, xs,
+    xout, ocols, z0, z1, z2, z3, z4, z5, z6, z7,
+    b_vm, a_vm, bs_vm, bc_vm, cols_vm, scale_vm, bsend, brecv, arecv, prods,
     idx_s, idx_r, as_s, as_r, idx_sm, as_sm, ctable, stable, msend, mrecv, m_sm,
-    local_sem, out_sem, msm_sem, idx_ss, idx_rs, as_ss, as_rs, b_ss, b_rs, m_ss, m_rs, a_ss, a_rs,
+    local_sem, msm_sem, idx_ss, idx_rs, as_ss, as_rs, b_ss, b_rs, m_ss, m_rs, a_ss, a_rs,
 ):
     c, r = lax.axis_index("col"), lax.axis_index("row")
     s, q = c // 2, c % 2
@@ -125,6 +125,13 @@
             eights = [jnp.broadcast_to(v[n:n + 1, :], (8, 128)) for n in range(4)]
             table[lanes, :] = jnp.transpose(jnp.concatenate(eights * 4, axis=0))
 
+    def clear(t, carry):
+        for acc in (z0, z1, z2, z3, z4, z5, z6, z7):
+            acc[pl.ds(pl.multiple_of(t * 64, 64), 64), :] = jnp.zeros((64, 128), F32)
+        return carry
+
+    lax.fori_loop(0, 64, clear, 0)
+
     for e in range(1, 8):
         sb, rb = (s + e) % 8, (r + 8 - e) % 8
         send(idx_s, idx_r.at[sb], idx_ss.at[e - 1], idx_rs.at[sb], dev(sb, q, rb)).wait_recv()
@@ -193,9 +200,6 @@
     low, high = group % 2 == 0, group < 2
     quarter = lax.broadcasted_iota(I32, (32, 128), 1) // 32
 
-    def out_copy(e):
-        return pltpu.make_async_copy(xs.at[e % 2], xout.at[e], out_sem.at[e])
-
     def scales_copy(e):
         sb, p = chip_behind(e), core(e)
         return pltpu.make_async_copy(mrecv.at[(sb + r) % 8, p], m_sm.at[e], msm_sem.at[e])
@@ -206,7 +210,7 @@
                 rows = [prods[e % 2, i, m * 32 + h * 8:m * 32 + h * 8 + 8, :] for h in range(4)]
                 for n, block in enumerate(lane_groups(rows, low, high)):
                     w = m * 4 + n
-                    xs[e % 2, i, w] = block * m_sm[e, 0, w * 8 + i]
+                    xout[e, i, w] = block * m_sm[e, 0, w * 8 + i]
 
     def process(e, carry, late=True):
         sb, p = chip_behind(e), core(e)
@@ -236,10 +240,6 @@
         if late:
             scales_copy(e - 1).wait()
 
-            @pl.when(e >= 3)
-            def _():
-                out_copy(e - 3).wait()
-
         if late:
             finish(e - 1)
         for i in range(8):
@@ -248,88 +248,75 @@
             left = jnp.concatenate([jnp.where(quarter == m, a, zero) for m in range(4)], axis=0)
             right = brecv[kb, p, i * 4:i * 4 + 4].reshape(128, 128)
             prods[e % 2, i] = jnp.dot(left, right, preferred_element_type=F32)
-        if late:
-            out_copy(e - 1).start()
         return carry
 
     process(0, 0, late=False)
     lax.fori_loop(1, 16, process, 0)
     scales_copy(15).wait()
-    out_copy(13).wait()
     finish(15)
-    out_copy(15).start()
     for copy in idx_sends + a_sends:
         copy.wait_send()
     for e in range(2, 18):
         if e != 16:
             for copy in to_peer(e):
                 copy.wait_send()
-    for e in (14, 15):
-        out_copy(e).wait()
-
-
-def scatter_kernel(cols, x_ref, out_ref, x, sem, *accs):
-    g = pl.program_id(0)
-
-    @pl.when(g == 0)
-    def _():
-        def load(e):
-            return pltpu.make_async_copy(x_ref.at[e], x.at[e], sem.at[e])
-
-        for e in range(16):
-            load(e).start()
-
-        def clear(t, _):
-            for acc in accs:
-                acc[pl.ds(pl.multiple_of(t * 64, 64), 64), :] = jnp.zeros((64, 128), F32)
-            return _
-
-        lax.fori_loop(0, 64, clear, 0)
-
-        def add(e, _):
-            load(e).wait()
-            for w in range(16):
-                at = [pl.ds(pl.multiple_of(cols[e, w * 8 + i], 8), 8) for i in range(8)]
-                new = [acc[at[i], :] + x[e, i, w] for i, acc in enumerate(accs)]
-                for i, acc in enumerate(accs):
-                    acc[at[i], :] = new[i]
-            return _
-
-        lax.fori_loop(0, 16, add, 0)
+
+
+def scatter_kernel(cols, x, *refs):
+    out_ref, accs, tiles, sem = refs[8], refs[9:17], refs[17], refs[18]
+
+    def add(e, _):
+        for w in range(16):
+            at = [pl.ds(pl.multiple_of(cols[e, w * 8 + i], 8), 8) for i in range(8)]
+            new = [acc[at[i], :] + x[e, i, w] for i, acc in enumerate(accs)]
+            for i, acc in enumerate(accs):
+                acc[at[i], :] = new[i]
+        return _
+
+    lax.fori_loop(0, 16, add, 0)
 
     group = lax.broadcasted_iota(I32, (16, 128), 1) // 32
     low, high = group % 2 == 0, group < 2
+
+    def out_copy(i, t):
+        lanes = pl.ds(pl.multiple_of(t * 2048, 2048), 2048)
+        return pltpu.make_async_copy(tiles.at[i, :, lanes], out_ref.at[i, :, lanes], sem.at[i, t])
+
     for i, acc in enumerate(accs):
-        @pl.when(g == i)
-        def _(acc=acc):
-            def tile(t, _):
-                for u in range(8):
-                    base = pl.multiple_of((t * 8 + u) * 64, 64)
-                    v = [
-                        jnp.concatenate([acc[pl.ds(base + n * 8, 8), :], acc[pl.ds(base + 32 + n * 8, 8), :]], axis=0).astype(BF16)
-                        for n in range(4)
-                    ]
-                    w = lane_groups(v, low, high)
-                    for h in range(4):
-                        lanes = pl.ds(pl.multiple_of((t * 8 + u) * 256, 256), 256)
-                        out_ref[0, h * 8:h * 8 + 8, lanes] = jnp.concatenate([w[h][0:8], w[h][8:16]], axis=1)
-                return _
-
-            lax.fori_loop(0, 8, tile, 0)
+        def tile(t, _):
+            for u in range(8):
+                base = pl.multiple_of((t * 8 + u) * 64, 64)
+                v = [
+                    jnp.concatenate([acc[pl.ds(base + n * 8, 8), :], acc[pl.ds(base + 32 + n * 8, 8), :]], axis=0).astype(BF16)
+                    for n in range(4)
+                ]
+                w = lane_groups(v, low, high)
+                for h in range(4):
+                    lanes = pl.ds(pl.multiple_of((t * 8 + u) * 256, 256), 256)
+                    tiles[i, h * 8:h * 8 + 8, lanes] = jnp.concatenate([w[h][0:8], w[h][8:16]], axis=1)
+            out_copy(i, t).start()
+            return _
+
+        lax.fori_loop(0, 8, tile, 0)
+    for i in range(8):
+        for t in range(8):
+            out_copy(i, t).wait()
 
 
 def on_device(a_blocks, a_scale, a_cols, b_blocks, b_scale, b_cols):
     hbm = pl.BlockSpec(memory_space=pltpu.HBM)
+    vmem = pl.BlockSpec(memory_space=pltpu.VMEM)
     dma = pltpu.SemaphoreType.DMA
-    x, cols = pl.pallas_call(
+    sums = jax.ShapeDtypeStruct((4096, 128), F32)
+    x, cols, *zeros = pl.pallas_call(
         exchange_kernel,
         name="exchange",
         out_shape=(
             jax.ShapeDtypeStruct((16, 8, 16, 8, 128), F32),
             jax.ShapeDtypeStruct((16, 128), I32),
-        ),
+        ) + (sums,) * 8,
         in_specs=[hbm] * 6,
-        out_specs=(hbm, pl.BlockSpec(memory_space=pltpu.VMEM)),
+        out_specs=(vmem,) * 10,
         scratch_shapes=[
             pltpu.VMEM((512, 32, 128), BF16),
             pltpu.VMEM((16, 32, 128), BF16),
@@ -341,7 +328,6 @@
             pltpu.VMEM((8, 2, 32, 32, 128), BF16),
             pltpu.VMEM((8, 2, 8, 32, 128), BF16),
             pltpu.VMEM((2, 8, 128, 128), F32),
-            pltpu.VMEM((2, 8, 16, 8, 128), F32),
             pltpu.VMEM((8, 128), I32),
             pltpu.VMEM((8, 8, 128), I32),
             pltpu.VMEM((8, 128), F32),
@@ -353,21 +339,21 @@
             pltpu.VMEM((16, 8, 128), F32),
             pltpu.VMEM((8, 2, 8, 128), F32),
             pltpu.SMEM((16, 8, 128), F32),
-            dma((10,)), dma((16,)), dma((16,)), dma((7,)), dma((8,)), dma((7,)), dma((8,)),
+            dma((10,)), dma((16,)), dma((7,)), dma((8,)), dma((7,)), dma((8,)),
             dma((16,)), dma((8, 2)), dma((16,)), dma((8, 2)), dma((9,)), dma((9,)),
         ],
-        compiler_params=pltpu.CompilerParams(collective_id=0, has_side_effects=True, vmem_limit_bytes=67043328),
-    )(a_cols[0, 0].T, a_scale[0, 0].T, a_blocks[0, 0], b_blocks[0, 0], b_scale[0, 0].T, b_cols[0, 0].T)
-    out = pl.pallas_call(
+        compiler_params=pltpu.CompilerParams(collective_id=0, has_side_effects=True, vmem_limit_bytes=24 << 20),
+    )(*[pltpu.with_memory_space_constraint(v, pltpu.HBM) for v in (a_cols[0, 0].T, a_scale[0, 0].T, a_blocks[0, 0], b_blocks[0, 0], b_scale[0, 0].T, b_cols[0, 0].T)])
+    out, *_ = pl.pallas_call(
         scatter_kernel,
         name="scatter",
-        grid=(8,),
-        out_shape=jax.ShapeDtypeStruct((8, 32, 16384), BF16),
-        in_specs=[pl.BlockSpec(memory_space=pltpu.SMEM), hbm],
-        out_specs=pl.BlockSpec((1, 32, 16384), lambda g: (g, 0, 0)),
-        scratch_shapes=[pltpu.VMEM((16, 8, 16, 8, 128), F32), dma((16,))] + [pltpu.VMEM((4096, 128), F32)] * 8,
-        compiler_params=pltpu.CompilerParams(vmem_limit_bytes=67043328),
-    )(cols, x)
+        out_shape=(jax.ShapeDtypeStruct((8, 32, 16384), BF16),) + (sums,) * 8,
+        input_output_aliases={n + 2: n + 1 for n in range(8)},
+        in_specs=[pl.BlockSpec(memory_space=pltpu.SMEM)] + [vmem] * 9,
+        out_specs=(hbm,) + (vmem,) * 8,
+        scratch_shapes=[pltpu.VMEM((8, 32, 16384), BF16), dma((8, 8))],
+        compiler_params=pltpu.CompilerParams(vmem_limit_bytes=24 << 20),
+    )(cols, x, *zeros)
     return out[None, None]
 
 

time: 86.8 us -> 82.9 us (0.955)
  Pallas kernels: 86.2 us -> 82.2 us
    pallas_call x1, Pallas kernels: 16.1 us -> 13.8 us  [on_device(): pl.pallas_call(scatter_kernel, name='scatter', out_shape=(jax.ShapeDtypeS...]
    pallas_call x1, Pallas kernels: 70.1 us -> 68.4 us  [on_device(): pl.pallas_call(exchange_kernel, name='exchange', out_shape=(jax.ShapeDtyp...]
where the time goes in v5:
time: 82.9 us; the launch traced here: 82.2 us
  Pallas kernels  82.2 us (99%)
    pallas_call x1, Pallas kernels, on_device(): pl.pallas_call(exchange_kernel, name='exchange', out_shape=(jax.ShapeDtyp...  68.4 us
    pallas_call x1, Pallas kernels, on_device(): pl.pallas_call(scatter_kernel, name='scatter', out_shape=(jax.ShapeDtypeS...  13.8 us

profile of v5, /device:TPU:31, one launch (start us, length us, event | category | flops | bytes accessed | tf_op | source)
XLA Modules:
  0.0 82.2 jit_solution(10858087022491075139)
XLA Ops:
  0.0 68.4 %exchange.1 = (f32[16,8,16,8,128]{4,3,2,1,0:T(8,128)S(1)}, s32[16,128]{1,0:T(8,128)S(1)}, f32[4096,128]{1,0:T(8,128)S(1)}, f32[4096,128]{1,0:T(8,128)S(1)}, f32[...) custom-call(s32[4,16]{1,0:T(4,128)} %bitcast.19, ...), custom_call_target="tpu_custom_call" | custom-call | tf_op jit(solution)/shard_map/exchange/pallas_call | solution.py:311
  68.4 13.8 %scatter.1 = (bf16[8,32,16384]{2,1,0:T(8,128)(2,1)}, f32[4096,128]{1,0:T(8,128)S(1)}, f32[4096,128]{1,0:T(8,128)S(1)}, f32[4096,128]{1,0:T(8,128)S(1)}, f32[4096...) custom-call(s32[16,128]{1,0:T(8,128)S(1)} %get-tuple-element.16.cols, ...), custom_call_target="tpu_custom_call", output_to_operand_aliasing={{1}: (2, {}), {2}: (3, {}), {3}: (4, {}), {4}: (5, {}), {5}... | custom-call | tf_op jit(solution)/shard_map/scatter/pallas_call | solution.py:347

commit v6 on v5

--- a/solution.py
+++ b/solution.py
@@ -77,17 +77,23 @@
         copy.start()
 
     barrier = pltpu.get_barrier_semaphore()
-    peers = []
-    for e in range(1, 8):
-        peers.append(dev((s + 8 - e) % 8, q, (r + e) % 8))
-    for e in range(1, 16):
-        peers.append(dev(chip(e), core(e), r))
+    def greet(peer):
+        pl.semaphore_signal(barrier, inc=1, device_id=peer, device_id_type=MESH)
+
+    def greet_diagonal(e, carry):
+        greet(dev((s + 8 - e) % 8, q, (r + e) % 8))
+        return carry
+
+    def greet_column(e, carry):
+        greet(dev(chip(e), core(e), r))
+        return carry
+
+    lax.fori_loop(1, 8, greet_diagonal, 0)
+    lax.fori_loop(1, 16, greet_column, 0)
     for p in range(2):
-        peers.append(dev(s, p, rx))
+        greet(dev(s, p, rx))
     for dy in HOPS:
-        peers.append(dev(s, q, row_at(dy)))
-    for peer in peers:
-        pl.semaphore_signal(barrier, inc=1, device_id=peer, device_id_type=MESH)
+        greet(dev(s, q, row_at(dy)))
     idx_s[...] = jnp.zeros_like(idx_s)
     as_s[...] = jnp.zeros_like(as_s)
     loads[0].wait()
@@ -96,7 +102,7 @@
         idx_s[p * 4:p * 4 + 4, 0:8] = cols_vm[:, p * 8:p * 8 + 8]
         as_s[p * 4:p * 4 + 4, 0:8] = scale_vm[:, p * 8:p * 8 + 8]
     loads[2].wait()
-    pl.semaphore_wait(barrier, len(peers))
+    pl.semaphore_wait(barrier, 27)
 
     idx_sends = []
     for e in range(1, 8):

time: 82.9 us -> 83 us (level)
  no operation moved by 1% of the time
where the time goes in v6:
time: 83 us; the launch traced here: 82.9 us
  Pallas kernels  82.9 us (100%)
    pallas_call x1, Pallas kernels, on_device(): pl.pallas_call(exchange_kernel, name='exchange', out_shape=(jax.ShapeDtyp...  69.1 us
    pallas_call x1, Pallas kernels, on_device(): pl.pallas_call(scatter_kernel, name='scatter', out_shape=(jax.ShapeDtypeS...  13.8 us

profile of v6, /device:TPU:31, one launch (start us, length us, event | category | flops | bytes accessed | tf_op | source)
XLA Modules:
  0.0 82.9 jit_solution(60841980491114010)
XLA Ops:
  0.0 69.1 %exchange.1 = (f32[16,8,16,8,128]{4,3,2,1,0:T(8,128)S(1)}, s32[16,128]{1,0:T(8,128)S(1)}, f32[4096,128]{1,0:T(8,128)S(1)}, f32[4096,128]{1,0:T(8,128)S(1)}, f32[...) custom-call(s32[4,16]{1,0:T(4,128)} %bitcast.19, ...), custom_call_target="tpu_custom_call" | custom-call | tf_op jit(solution)/shard_map/exchange/pallas_call | solution.py:317
  69.1 13.8 %scatter.1 = (bf16[8,32,16384]{2,1,0:T(8,128)(2,1)}, f32[4096,128]{1,0:T(8,128)S(1)}, f32[4096,128]{1,0:T(8,128)S(1)}, f32[4096,128]{1,0:T(8,128)S(1)}, f32[4096...) custom-call(s32[16,128]{1,0:T(8,128)S(1)} %get-tuple-element.16.cols, ...), custom_call_target="tpu_custom_call", output_to_operand_aliasing={{1}: (2, {}), {2}: (3, {}), {3}: (4, {}), {4}: (5, {}), {5}... | custom-call | tf_op jit(solution)/shard_map/scatter/pallas_call | solution.py:353
